TPU v7x, 32 devices: a whole 2x2x4 slice. The times are simulated.
32 devices in a mesh: dp: 8 (over z, x), seq: 4 (over y, core).
Axes of the slice: x: 2, y: 2, z: 4, core: 2. Of those that a mesh axis runs over, the one named last changes fastest.
Arguments:
- query: bfloat16 [8, 1024, 2048], P('dp', 'seq'), may hold values from -6 to 6
- keys: bfloat16 [8, 1024, 256], P('dp', 'seq'), may hold values from -6 to 6
- values: bfloat16 [8, 1024, 256], P('dp', 'seq'), may hold values from -6 to 6
- grad_out: bfloat16 [8, 1024, 2048], P('dp', 'seq'), may hold values from -6 to 6
- layer_input: bfloat16 [8, 1024, 1536], P('dp', 'seq'), may hold values from -6 to 6
- sinks: float32 [32], replicated, may hold values from 1 to 5
- segments: int32 [8, 1024], P('dp', 'seq'), may hold values from 0 to 255, as said below
- positions: int32 [8, 1024], P('dp', 'seq'), may hold values from 0 to 8191, as said below
Outputs:
- grad_query: bfloat16 [8, 1024, 2048], P('dp', 'seq')
- weight_grads: float32 [1536, 256], P('dp')
Inputs may be any that keep to these rules, and one draw needn't show every extreme that they name: `segments`: segment ids never fall along a span. positions rise by one inside a document.
All inputs are finite; a program needn't handle non-finite values.
Results may differ from a plain program's by a relative error of at most 0.0086.
Values may be sent and summed in bfloat16 or wider, within the bound.
No kernel may reach another device: no remote copies, remote signals or barrier semaphores. Data moves between devices by JAX's collectives and lax.ppermute only.
A program may use at most 64 MiB of HBM per device.

v0:
```python
import jax
import jax.numpy as jnp
from jax import lax
from jax.sharding import PartitionSpec as P

HEADDIM = 64
WINDOW = 128


theta_base = 150000.0
seg_modulus = 256


def from_behind(shard, axis, by):
    count = lax.axis_size(axis)
    pairs = [(i, i + by) for i in range(count) if 0 <= i + by < count]
    return lax.ppermute(shard, axis, pairs)


def rotate_back(grads, token_pos):
    half_dim = grads.shape[-1] // 2
    frequency = theta_base ** (-(jnp.arange(half_dim, dtype=jnp.float32) * 2.0 / grads.shape[-1]))
    angles = token_pos.astype(jnp.float32)[:, None] * frequency[None, :]
    cosine = jnp.cos(angles)[:, None, :]
    sine_val = jnp.sin(angles)[:, None, :]
    lower_half = grads[..., :half_dim]
    upper_half = grads[..., half_dim:]
    return jnp.concatenate(
        [lower_half * cosine + upper_half * sine_val, upper_half * cosine - lower_half * sine_val],
        axis=-1,
    )


def body(query, keys, values, grad_out, layer_input, sinks, segments, positions):
    query = query[0]
    keys = keys[0]
    values = values[0]
    grad_out = grad_out[0]
    layer_input = layer_input[0]
    segments = segments[0]
    positions = positions[0]
    tok_rows = query.shape[0]
    head_dim = HEADDIM
    heads_q = sinks.shape[0]
    heads_kv = keys.shape[1] // head_dim
    group = heads_q // heads_kv
    width = WINDOW
    scale = 1.0 / head_dim**0.5
    seg_local = jnp.remainder(segments, seg_modulus).astype(jnp.float32)
    rim_keys, rim_values, rim_segs = from_behind(
        (
            keys[tok_rows - width :],
            values[tok_rows - width :],
            seg_local[tok_rows - width :].astype(jnp.bfloat16),
        ),
        "seq",
        1,
    )
    all_keys = jnp.concatenate([rim_keys, keys], axis=0)
    all_values = jnp.concatenate([rim_values, values], axis=0)
    key_segs = jnp.concatenate([rim_segs.astype(jnp.float32), seg_local], axis=0)
    seq_index = lax.axis_index("seq")
    query_idx = jnp.arange(tok_rows)[:, None] + width
    key_idx = jnp.arange(tok_rows + width)[None, :]
    offset = query_idx - key_idx
    allowed = (offset >= 0) & (offset < width) & (seg_local[:, None] == key_segs[None, :])
    allowed = allowed & ((key_idx >= width) | (seq_index > 0))
    allowed = allowed[None]
    query_parts = []
    key_parts = []
    for head_group in range(heads_kv):
        low_col = head_group * group * head_dim
        high_col = low_col + group * head_dim
        q_grp = query[:, low_col:high_col].reshape(tok_rows, group, head_dim)
        g_grp = grad_out[:, low_col:high_col].reshape(tok_rows, group, head_dim)
        k_grp = all_keys[:, head_group * head_dim : (head_group + 1) * head_dim]
        v_grp = all_values[:, head_group * head_dim : (head_group + 1) * head_dim]
        scores = jnp.einsum("qhd,kd->hqk", q_grp, k_grp, preferred_element_type=jnp.float32) * scale
        sink_col = sinks[head_group * group : (head_group + 1) * group][:, None, None]
        masked = jnp.where(allowed, scores, -jnp.inf)
        peak = jnp.maximum(jnp.max(masked, axis=-1, keepdims=True), sink_col)
        expo = jnp.where(allowed, jnp.exp(masked - peak), 0.0)
        total = jnp.sum(expo, axis=-1, keepdims=True) + jnp.exp(sink_col - peak)
        probs = expo / total
        grad_probs = jnp.einsum("qhd,kd->hqk", g_grp, v_grp, preferred_element_type=jnp.float32)
        delta = jnp.sum(probs * grad_probs, axis=-1, keepdims=True)
        grad_scores = probs * (grad_probs - delta)
        grad_b = grad_scores.astype(jnp.bfloat16)
        grad_q = (
            jnp.einsum("hqk,kd->qhd", grad_b, k_grp, preferred_element_type=jnp.float32) * scale
        )
        query_parts.append(grad_q.reshape(tok_rows, group * head_dim).astype(jnp.bfloat16))
        key_parts.append(
            jnp.einsum("hqk,qhd->kd", grad_b, q_grp, preferred_element_type=jnp.float32) * scale
        )
    grad_query = jnp.concatenate(query_parts, axis=-1)
    key_grads = jnp.concatenate(key_parts, axis=-1)
    back_keys = from_behind(key_grads[:width].astype(jnp.bfloat16), "seq", -1).astype(jnp.float32)
    local_keys = key_grads[width:]
    local_keys = jnp.concatenate(
        [local_keys[: tok_rows - width], local_keys[tok_rows - width :] + back_keys], axis=0
    )
    turned = rotate_back(local_keys.reshape(tok_rows, heads_kv, head_dim), positions)
    k_grads = turned.reshape(tok_rows, heads_kv * head_dim).astype(jnp.bfloat16)
    shard = lax.psum_scatter(
        lax.dot_general(
            layer_input, k_grads, (((0,), (0,)), ((), ())), preferred_element_type=jnp.float32
        ),
        "dp",
        scatter_dimension=0,
        tiled=True,
    )
    shard = lax.psum(shard, "seq")
    return (grad_query[None], shard)


def solution(mesh):
    return jax.shard_map(
        body,
        mesh=mesh,
        in_specs=(
            P("dp", "seq", None),
            P("dp", "seq", None),
            P("dp", "seq", None),
            P("dp", "seq", None),
            P("dp", "seq", None),
            P(),
            P("dp", "seq"),
            P("dp", "seq"),
        ),
        out_specs=(P("dp", "seq", None), P("dp", None)),
        check_vma=False,
    )
```

profile of v0, /device:TPU:0, one launch (start us, length us, event | category | flops | bytes accessed | tf_op | source)
XLA Modules:
  0.0 173.2 jit_solution(16358544082177896071)
XLA Ops:
  7.2 0.8 fusion.83
  8.6 2.9 %collective-permute-start.1 = (bf16[128]{0:T(256)(128)(2,1)}, bf16[128]{0:T(256)(128)(2,1)}, u32[]{:S(2)}, u32[]{:S(2)}) collective-permute-start(bf16[128]{0:T(256)(128)(2,1)} %slice.98), channel_id=1, source_target_pairs={{0,1},{1,2},{2,3},{4,5},{5,6},{6,7},{8,9},{9,10},{10,11},{12,13},{... | collective-permute-start | bytes 776 | tf_op jit(solution)/shard_map/ppermute | solution.py:17
  11.5 1.0 copy.35
  12.5 0.6 slice_bitcast_fusion.1
  13.2 4.0 %collective-permute-start = (bf16[128,256]{0,1:T(8,128)(2,1)}, bf16[128,256]{0,1:T(8,128)(2,1)S(1)}, u32[]{:S(2)}, u32[]{:S(2)}) collective-permute-start(bf16[128,256]{0,1:T(8,128)(2,1)} %slice_bitcast_fusion.1), channel_id=1, source_target_pairs={{0,1},{1,2},{2,3},{4,5},{5,6},{6,7},{8,9},{9,10},{10,11},{12,13},{... | collective-permute-start | bytes 196616 | tf_op jit(solution)/shard_map/ppermute | solution.py:17
  17.2 1.0 copy.38
  18.2 0.6 slice_bitcast_fusion
  18.8 1.9 %collective-permute-start.2 = (bf16[128,256]{0,1:T(8,128)(2,1)}, bf16[128,256]{0,1:T(8,128)(2,1)S(1)}, u32[]{:S(2)}, u32[]{:S(2)}) collective-permute-start(bf16[128,256]{0,1:T(8,128)(2,1)} %slice_bitcast_fusion), channel_id=1, source_target_pairs={{0,1},{1,2},{2,3},{4,5},{5,6},{6,7},{8,9},{9,10},{10,11},{12,13},{... | collective-permute-start | bytes 196616 | tf_op jit(solution)/shard_map/ppermute | solution.py:17
  20.7 0.6 negate_power_fusion
  21.9 0.6 fusion.70
  22.4 1.2 convert_element_type.102
  23.7 1.3 fusion.88
  25.0 1.3 fusion.85
  26.9 0.9 fusion.86
  27.8 1.1 copy.40
  28.8 1.8 %copy.49 = bf16[256,512]{0,1:T(8,128)(2,1)} copy(bf16[256,512]{1,0:T(8,128)(2,1)} %get-tuple-element.22) | data formatting | bytes 524288 | tf_op jit(solution)/shard_map/slice | solution.py:75
  30.6 1.8 %copy.46 = bf16[256,512]{0,1:T(8,128)(2,1)} copy(bf16[256,512]{1,0:T(8,128)(2,1)} %get-tuple-element.23) | data formatting | bytes 524288 | tf_op jit(solution)/shard_map/slice | solution.py:75
  32.4 0.8 copy.43
  33.3 0.6 convert_element_type.84
  33.9 0.9 fusion.37
  34.8 0.6 fusion.89
  35.4 0.7 fusion.12
  36.1 0.8 fusion.17
  36.9 0.6 fusion.62
  37.5 0.6 fusion.68
  38.1 2.5 %fusion.9 = (f32[8,256]{1,0:T(8,128)S(1)}, f32[8,256]{1,0:T(8,128)S(1)}, f32[8,256]{1,0:T(8,128)S(1)}, f32[8,256]{1,0:T(8,128)S(1)}, f32[384,256,8]{1,0,2:T(8,128)S(1)}) fusion(f32[8,256]{1,0:T(8,128)S(1)} %exponential_add_fusion.3, f32[8,256]{1,0:T(8,128)S(1)} %broadcast_maximum_fusion.3, f32[384,256,8]{1,0,2:T(8,128)S(1)} %get-tuple-element.41, ...), kind=kOutput, calls=%fused_computation.20 | convolution fusion | flops 113336320 | bytes 16334848 | tf_op jit(solution)/shard_map/qhd,kd->hqk/dot_general | solution.py:85
  40.7 2.0 %fusion.11 = (bf16[8,256,384]{1,2,0:T(8,128)(2,1)S(1)}, f32[8,256]{1,0:T(8,128)S(1)}) fusion(f32[384,256,8]{1,0,2:T(8,128)S(1)} %get-tuple-element.42, f32[8,256]{1,0:T(8,128)S(1)} %get-tuple-element.6, f32[8,256]{1,0:T(8,128)S(1)} %exponential_add_fusion.3, f32[8,256]{1,0:T(8,128)S(1)} %broadcast_maximum_fusion.3, f32[384,256,8]{1,0,2:T(8,128)S(1)} %get-tuple-element.41, ...), kind=kLoop, calls=%fused_computation.22 | loop fusion | flops 10221568 | bytes 11149312 | tf_op jit(solution)/shard_map/convert_element_type | solution.py:88
  42.7 0.6 fusion.31
  43.5 2.8 %fusion.6 = (f32[8,256]{1,0:T(8,128)S(1)}, f32[8,256]{1,0:T(8,128)S(1)}, f32[8,256]{1,0:T(8,128)S(1)}, f32[384,256,8]{1,0,2:T(8,128)S(1)}) fusion(f32[8,256]{1,0:T(8,128)S(1)} %exponential_add_fusion.2, f32[8,256]{1,0:T(8,128)S(1)} %broadcast_maximum_fusion.2, f32[384,256,8]{1,0,2:T(8,128)S(1)} %fusion.62, pred[256,384]{0,1:T(8,128)(4,1)S(1)} %fusion.37, ...), kind=kOutput, calls=%fused_computation.14 | convolution fusion | flops 114124800 | bytes 13197312 | tf_op jit(solution)/shard_map/qhd,kd->hqk/dot_general | solution.py:85
  46.4 0.6 fusion.57
  47.2 2.2 %fusion.3 = (f32[8,256]{1,0:T(8,128)S(1)}, f32[8,256]{1,0:T(8,128)S(1)}, f32[384,256,8]{1,0,2:T(8,128)S(1)}) fusion(f32[8,256]{1,0:T(8,128)S(1)} %get-tuple-element.46, f32[8,256]{1,0:T(8,128)S(1)} %broadcast_maximum_fusion.1, f32[384,256,8]{1,0,2:T(8,128)S(1)} %fusion.68, pred[256,384]{0,1:T(8,128)(4,1)S(1)} %fusion.37, f32[384,256,8]{1,0,2:T(8,128)S(1)} %fusion.57, ...), kind=kOutput, calls=%fused_computation.8 | convolution fusion | flops 111767552 | bytes 13189120 | tf_op jit(solution)/shard_map/qhd,kd->hqk/dot_general | solution.py:85
  49.5 3.6 %fusion.8 = (bf16[8,256,384]{1,2,0:T(8,128)(2,1)S(1)}, bf16[8,256,384]{1,2,0:T(8,128)(2,1)S(1)}, bf16[8,256,384]{1,2,0:T(8,128)(2,1)S(1)}) fusion(f32[384,256,8]{1,0,2:T(8,128)S(1)} %get-tuple-element.43, f32[8,256]{1,0:T(8,128)S(1)} %get-tuple-element.10, f32[8,256]{1,0:T(8,128)S(1)} %exponential_add_fusion.2, f32[8,256]{1,0:T(8,128)S(1)} %broadcast_maximum_fusion.2, ...), kind=kLoop, calls=%fused_computation.16 | loop fusion | flops 18874368 | bytes 23764992 | tf_op jit(solution)/shard_map/convert_element_type | solution.py:88
  53.2 0.6 fusion.29
  53.8 0.6 fusion.28
  54.4 0.6 fusion.30
  55.3 1.3 collective-permute-start.3
  56.8 1.6 collective-permute-done.3
  58.5 1.5 convolution_bitcast_fusion
  60.1 3.1 %copy.68 = f32[1536,256]{1,0:T(8,128)} copy(f32[1536,256]{0,1:T(8,128)} %convolution_bitcast_fusion) | data formatting | bytes 3145728
  63.7 1.9 %fusion.26 = bf16[64,8,256]{2,0,1:T(8,128)(2,1)S(1)} fusion(bf16[8,256,384]{1,2,0:T(8,128)(2,1)} %copy-done.4, bf16[256,256]{0,1:T(8,128)(2,1)S(1)} %bitcast.210, bf16[128,256]{0,1:T(8,128)(2,1)S(1)} %collective-permute-done), kind=kOutput, calls=%fused_computation.47 | convolution fusion | flops 101023744 | bytes 2031616 | tf_op jit(solution)/shard_map/hqk,kd->qhd/dot_general | solution.py:90
  65.8 2.5 %fusion.25 = bf16[64,8,256]{2,0,1:T(8,128)(2,1)} fusion(bf16[8,256,384]{1,2,0:T(8,128)(2,1)} %copy-done.3, bf16[256,256]{0,1:T(8,128)(2,1)S(1)} %bitcast.211, bf16[128,256]{0,1:T(8,128)(2,1)S(1)} %collective-permute-done), kind=kOutput, calls=%fused_computation.46 | convolution fusion | flops 101023744 | bytes 2031616 | tf_op jit(solution)/shard_map/hqk,kd->qhd/dot_general | solution.py:90
  68.3 1.1 copy.52
  69.4 1.2 fusion.27
  70.8 60.4 %reduce-scatter.4.cloned.1.call-done = f32[192,256]{1,0:T(8,128)} async-done(((f32[1536,256]{1,0:T(8,128)}), f32[192,256]{1,0:T(8,128)}) %reduce-scatter.4.cloned.1.call-update) | async-done | bytes 196624
  131.2 1.8 %copy.69 = f32[192,256]{0,1:T(8,128)} copy(f32[192,256]{1,0:T(8,128)} %reduce-scatter.4.cloned.1.call-done) | data formatting | bytes 393216
  133.0 1.1 maximum_bitcast_fusion
  134.1 30.6 %all-reduce.2.cloned.1.call-done = f32[192,256]{0,1:T(8,128)} async-done(((f32[192,256]{0,1:T(8,128)}), f32[192,256]{0,1:T(8,128)}) %all-reduce.2.cloned.1.call-update) | async-done | bytes 196624 | tf_op jit(solution)/shard_map/psum | solution.py:113
  164.7 1.7 %copy.59 = f32[192,256]{1,0:T(8,128)} copy(f32[192,256]{0,1:T(8,128)} %all-reduce.2.cloned.1.call-done) | data formatting | bytes 393216
  (63 shorter events, 4.0 us)
Async XLA Ops:
  7.2 51.4 %copy-start = (bf16[1,256,1536]{2,1,0:T(8,128)(2,1)S(1)}, bf16[1,256,1536]{2,1,0:T(8,128)(2,1)}, u32[]{:S(2)}) copy-start(bf16[1,256,1536]{2,1,0:T(8,128)(2,1)} %param.12) | copy-start | bytes 2359300
  7.2 19.7 %copy-start.8 = (bf16[1,256,2048]{2,1,0:T(8,128)(2,1)S(1)}, bf16[1,256,2048]{2,1,0:T(8,128)(2,1)}, u32[]{:S(2)}) copy-start(bf16[1,256,2048]{2,1,0:T(8,128)(2,1)} %param.11) | copy-start | bytes 3145732
  7.2 124.0 %reduce-scatter.4.cloned.1.call-start = ((), (), s32[]{:S(2)}) async-start(), calls=%async_computation.2 | async-start | bytes 1769472
  8.6 24.6 %collective-permute-start.1 = (bf16[128]{0:T(256)(128)(2,1)}, bf16[128]{0:T(256)(128)(2,1)}, u32[]{:S(2)}, u32[]{:S(2)}) collective-permute-start(bf16[128]{0:T(256)(128)(2,1)} %slice.98), channel_id=1, source_target_pairs={{0,1},{1,2},{2,3},{4,5},{5,6},{6,7},{8,9},{9,10},{10,11},{12,13},{... | collective-permute-start | bytes 776 | tf_op jit(solution)/shard_map/ppermute | solution.py:17
  13.2 21.6 %collective-permute-start = (bf16[128,256]{0,1:T(8,128)(2,1)}, bf16[128,256]{0,1:T(8,128)(2,1)S(1)}, u32[]{:S(2)}, u32[]{:S(2)}) collective-permute-start(bf16[128,256]{0,1:T(8,128)(2,1)} %slice_bitcast_fusion.1), channel_id=1, source_target_pairs={{0,1},{1,2},{2,3},{4,5},{5,6},{6,7},{8,9},{9,10},{10,11},{12,13},{... | collective-permute-start | bytes 196616 | tf_op jit(solution)/shard_map/ppermute | solution.py:17
  18.8 19.3 %collective-permute-start.2 = (bf16[128,256]{0,1:T(8,128)(2,1)}, bf16[128,256]{0,1:T(8,128)(2,1)S(1)}, u32[]{:S(2)}, u32[]{:S(2)}) collective-permute-start(bf16[128,256]{0,1:T(8,128)(2,1)} %slice_bitcast_fusion), channel_id=1, source_target_pairs={{0,1},{1,2},{2,3},{4,5},{5,6},{6,7},{8,9},{9,10},{10,11},{12,13},{... | collective-permute-start | bytes 196616 | tf_op jit(solution)/shard_map/ppermute | solution.py:17
  26.4 8.9 %copy-start.5 = (bf16[256,512]{0,1:T(8,128)(2,1)}, bf16[256,512]{0,1:T(8,128)(2,1)S(1)}, u32[]{:S(2)}) copy-start(bf16[256,512]{0,1:T(8,128)(2,1)S(1)} %copy.48) | copy-start | bytes 786436
  34.8 1.3 copy-start.9
  34.8 1.3 copy-start.12
  40.7 2.8 %copy-start.11 = (bf16[256,512]{0,1:T(8,128)(2,1)S(1)}, bf16[256,512]{0,1:T(8,128)(2,1)}, u32[]{:S(2)}) copy-start(bf16[256,512]{0,1:T(8,128)(2,1)} %copy.43) | copy-start | bytes 786436
  43.5 2.9 %copy-start.7 = (bf16[256,512]{0,1:T(8,128)(2,1)S(1)}, bf16[256,512]{0,1:T(8,128)(2,1)}, u32[]{:S(2)}) copy-start(bf16[256,512]{0,1:T(8,128)(2,1)} %copy.49) | copy-start | bytes 786436
  46.3 1.0 copy-start.10
  49.5 4.3 %copy-start.6 = (bf16[256,512]{0,1:T(8,128)(2,1)S(1)}, bf16[256,512]{0,1:T(8,128)(2,1)}, u32[]{:S(2)}) copy-start(bf16[256,512]{0,1:T(8,128)(2,1)} %copy-done.5) | copy-start | bytes 786436
  53.1 1.9 %copy-start.1 = (bf16[8,256,384]{1,2,0:T(8,128)(2,1)}, bf16[8,256,384]{1,2,0:T(8,128)(2,1)S(1)}, u32[]{:S(2)}) copy-start(bf16[8,256,384]{1,2,0:T(8,128)(2,1)S(1)} %get-tuple-element.32) | copy-start | bytes 4718596
  53.1 1.9 %copy-start.3 = (bf16[8,256,384]{1,2,0:T(8,128)(2,1)}, bf16[8,256,384]{1,2,0:T(8,128)(2,1)S(1)}, u32[]{:S(2)}) copy-start(bf16[8,256,384]{1,2,0:T(8,128)(2,1)S(1)} %get-tuple-element.31) | copy-start | bytes 4718596
  53.1 2.1 %copy-start.4 = (bf16[8,256,384]{1,2,0:T(8,128)(2,1)}, bf16[8,256,384]{1,2,0:T(8,128)(2,1)S(1)}, u32[]{:S(2)}) copy-start(bf16[8,256,384]{1,2,0:T(8,128)(2,1)S(1)} %get-tuple-element.33) | copy-start | bytes 4718596
  53.2 3.4 %copy-start.13 = (f32[1,256]{1,0:T(1,128)S(1)}, f32[1,256]{1,0:T(1,128)}, u32[]{:S(2)}) copy-start(f32[1,256]{1,0:T(1,128)} %convert_element_type.102) | copy-start | bytes 3076
  53.2 3.4 %copy-start.14 = (f32[32]{0:T(128)S(1)}, f32[32]{0:T(128)}, u32[]{:S(2)}) copy-start(f32[32]{0:T(128)} %negate_power_fusion) | copy-start | bytes 388
  55.3 3.1 %collective-permute-start.3 = (bf16[128,256]{0,1:T(8,128)(2,1)S(1)}, bf16[128,256]{0,1:T(8,128)(2,1)S(1)}, u32[]{:S(2)}, u32[]{:S(2)}) collective-permute-start(bf16[128,256]{0,1:T(8,128)(2,1)S(1)} %slice.226), channel_id=1, source_target_pairs={{1,0},{2,1},{3,2},{5,4},{6,5},{7,6},{9,8},{10,9},{11,10},{13,12},{... | collective-permute-start | bytes 196616 | tf_op jit(solution)/shard_map/ppermute | solution.py:17
  63.1 101.5 %all-reduce.2.cloned.1.call-start = ((), (), s32[]{:S(2)}) async-start(), calls=%async_computation.1 | async-start | bytes 524288 | tf_op jit(solution)/shard_map/psum | solution.py:113
  63.6 5.8 %copy-start.2 = (bf16[8,256,384]{1,2,0:T(8,128)(2,1)S(1)}, bf16[8,256,384]{1,2,0:T(8,128)(2,1)}, u32[]{:S(2)}) copy-start(bf16[8,256,384]{1,2,0:T(8,128)(2,1)} %copy-done.1) | copy-start | bytes 4718596
Sparse Core Ops, SparseCore 0:
  63.3 67.8 reduce-scatter.3
  133.5 31.1 all-reduce.1
where the time goes:
time: 174 us; the launch traced here: 173 us
  waiting for transfers between devices  92.7 us (53%)
  local copies, waits for them, and re-layouts  22 us (13%)
  matrix products  20.4 us (12%)
  between operations  14.5 us (8%)
  other arithmetic  13.5 us (8%)
  starting transfers between devices  10.2 us (6%)
    unnamed x3, waiting for transfers between devices  60.4 us
    psum x1, waiting for transfers between devices, body(): shard = lax.psum(shard, 'seq')  30.6 us
    ppermute x4, starting transfers between devices, from_behind(): return lax.ppermute(shard, axis, pairs)  10.1 us
    unnamed x35, local copies, waits for them, and re-layouts  9.09 us
    dot_general x4, matrix products, body(): jnp.einsum('qhd,kd->hqk', g_grp, v_grp, preferred_element_type=jnp.float32)  8.07 us
    slice x5, local copies, waits for them, and re-layouts, body(): g_grp = grad_out[:, low_col:high_col].reshape(tok_rows, group, head_dim)  6.38 us
    dot_general x4, matrix products, body(): jnp.einsum('hqk,kd->qhd', grad_b, k_grp, preferred_element_type=jnp.float32)  6.01 us
    convert_element_type x2, other arithmetic, body(): grad_b = grad_scores.astype(jnp.bfloat16)  5.62 us
  transfers between devices with their start and end apart: 6, of which 3 were waited for; matrix products, arithmetic and copies ran while one was open for 17% of the time, Pallas kernels for 0%

commit v1 on v0

v1 whole, which is shorter than its diff:
```python
import jax
import jax.numpy as jnp
import numpy as np
from jax import lax
from jax.experimental import pallas as pl
from jax.experimental.pallas import tpu as pltpu
from jax.sharding import PartitionSpec as P

HEADDIM = 64
WINDOW = 128
THETA = 150000.0
LOW = -1e30

F32 = jnp.float32
BF16 = jnp.bfloat16


def dot(a, b, ca, cb):
    return lax.dot_general(a, b, (((ca,), (cb,)), ((), ())), preferred_element_type=F32)


def iota(shape, dim):
    return lax.broadcasted_iota(jnp.int32, shape, dim)


def sin_cos(angle):
    turns = jnp.floor(angle * np.float32(2.0 / np.pi) + np.float32(0.5))
    rest = angle - turns * np.float32(1.5703125)
    rest = rest - turns * np.float32(4.837512969970703125e-4)
    rest = rest - turns * np.float32(7.54978995489188216e-8)
    sq = rest * rest
    sin_part = np.float32(-1.9515295891e-4) * sq + np.float32(8.3321608736e-3)
    sin_part = (sin_part * sq + np.float32(-1.6666654611e-1)) * sq * rest + rest
    cos_part = np.float32(2.443315711809948e-5) * sq + np.float32(-1.388731625493765e-3)
    cos_part = (cos_part * sq + np.float32(4.166664568298827e-2)) * sq * sq
    cos_part = cos_part - np.float32(0.5) * sq + np.float32(1.0)
    quadrant = turns.astype(jnp.int32)
    odd = (quadrant & 1) == 1
    sine = jnp.where(odd, cos_part, sin_part)
    cosine = jnp.where(odd, sin_part, cos_part)
    sine = jnp.where((quadrant & 2) == 2, -sine, sine)
    cosine = jnp.where(((quadrant + 1) & 2) == 2, -cosine, cosine)
    return sine, cosine


def as_column(row):
    return jnp.broadcast_to(row, (row.shape[1], row.shape[1])).T


def attention_kernel(
    group, n_kv, sinks_ref, first_ref, query_ref, grad_ref, keys_ref, values_ref,
    rim_keys_ref, rim_values_ref, rim_aux_ref, segs_ref, pos_ref, freq_ref,
    dq_ref, dk_ref, keys2, values2, keys_t, bias, acc, dk_all,
):
    kv = pl.program_id(0)
    w = WINDOW
    rows = query_ref.shape[0]
    blocks = rows // w
    lanes = 2 * HEADDIM
    lower = iota((w, lanes), 1) < HEADDIM
    tri = iota((w, w), 0) <= iota((w, w), 1)

    @pl.when(kv == 0)
    def _():
        rim_segs = rim_aux_ref[0:1, rim_aux_ref.shape[1] - w :].astype(F32)
        rim_segs = jnp.where(first_ref[0] == 0, np.float32(-1.0), rim_segs)
        segs = [rim_segs]
        for b in range(blocks):
            segs.append(segs_ref[0:1, b * w : (b + 1) * w].astype(F32))
        columns = [as_column(s) for s in segs]
        for b in range(blocks):
            key_segs = jnp.where(tri, columns[b + 1], columns[b])
            bias[b] = jnp.where(key_segs == segs[b + 1], np.float32(0.0), np.float32(LOW))

    own_half = (iota((w, lanes), 1) < HEADDIM) == ((kv % 2) == 0)
    for b in range(blocks + 1):
        if b == 0:
            k_tile, v_tile = rim_keys_ref[...], rim_values_ref[...]
        else:
            k_tile = keys_ref[(b - 1) * w : b * w, :]
            v_tile = values_ref[(b - 1) * w : b * w, :]
        k_tile = k_tile.astype(F32) * np.float32(HEADDIM**-0.5)
        v_tile = v_tile.astype(F32)
        k_tile = jnp.where(own_half, k_tile, pltpu.roll(k_tile, HEADDIM, 1))
        v_tile = jnp.where(own_half, v_tile, pltpu.roll(v_tile, HEADDIM, 1))
        keys2[b * w : (b + 1) * w, :] = k_tile.astype(BF16)
        values2[b * w : (b + 1) * w, :] = v_tile.astype(BF16)
        keys_t[:, b * w : (b + 1) * w] = k_tile.T[:HEADDIM].astype(BF16)

    tri2 = jnp.concatenate([tri, tri], axis=1)
    left = iota((1, 2 * w), 1) < w
    zero = jnp.zeros((), BF16)
    for b in range(blocks):
        key_win = keys2[b * w : (b + 2) * w, :]
        value_win = values2[b * w : (b + 2) * w, :]
        keyt_win = keys_t[:, b * w : (b + 2) * w]
        bias2 = jnp.concatenate([bias[b], bias[b]], axis=1)
        total_dk = None
        for pair in range(group // 2):
            q_tile = query_ref[b * w : (b + 1) * w, pair * lanes : (pair + 1) * lanes]
            g_tile = grad_ref[b * w : (b + 1) * w, pair * lanes : (pair + 1) * lanes]
            q2 = jnp.concatenate([jnp.where(lower, q_tile, zero), jnp.where(lower, zero, q_tile)], 0)
            g2 = jnp.concatenate([jnp.where(lower, g_tile, zero), jnp.where(lower, zero, g_tile)], 0)
            scores = dot(key_win, q2, 1, 1)
            scores = jnp.where(tri2, scores[w:], scores[:w]) + bias2
            head = kv * group + 2 * pair
            sink = jnp.where(left, sinks_ref[head], sinks_ref[head + 1])
            peak = jnp.maximum(jnp.max(scores, axis=0, keepdims=True), sink)
            expo = jnp.exp(scores - peak)
            total = jnp.sum(expo, axis=0, keepdims=True) + jnp.exp(sink - peak)
            probs = expo * (np.float32(1.0) / total)
            grad_probs = dot(value_win, g2, 1, 1)
            grad_probs = jnp.where(tri2, grad_probs[w:], grad_probs[:w])
            delta = jnp.sum(probs * grad_probs, axis=0, keepdims=True)
            ds = probs * (grad_probs - delta)
            ds_prev = jnp.where(tri2, np.float32(0.0), ds).astype(BF16)
            ds_cur = jnp.where(tri2, ds, np.float32(0.0)).astype(BF16)
            ds_win = jnp.concatenate([ds_prev, ds_cur], axis=0)
            part = dot(ds_win, q2, 1, 0)
            total_dk = part if total_dk is None else total_dk + part
            dq_t = dot(keyt_win, ds_win, 1, 0)
            dq_t = jnp.concatenate([dq_t[:, :w], dq_t[:, w:]], axis=0)
            dq_ref[b * w : (b + 1) * w, pair * lanes : (pair + 1) * lanes] = dq_t.T.astype(BF16)
        if b == 0:
            acc[0 : 2 * w, :] = total_dk
        else:
            acc[b * w : (b + 1) * w, :] += total_dk[:w]
            acc[(b + 1) * w : (b + 2) * w, :] = total_dk[w:]

    for tile in range(n_kv // 2):
        for odd in range(2):

            @pl.when(kv == 2 * tile + odd)
            def _(tile=tile, odd=odd):
                both = acc[...]
                both = (both + pltpu.roll(both, HEADDIM, 1)) * np.float32(HEADDIM**-0.5)
                cols = slice(tile * lanes, (tile + 1) * lanes)
                if odd == 0:
                    dk_all[:, cols] = both
                else:
                    low = iota(both.shape, 1) < HEADDIM
                    dk_all[:, cols] = jnp.where(low, dk_all[:, cols], both)

    @pl.when(kv == n_kv - 1)
    def _():
        half = HEADDIM // 2
        low = (iota((w, lanes), 1) % HEADDIM) < half
        for b in range(blocks + 1):
            if b == 0:
                pos = (
                    rim_aux_ref[1:2, rim_aux_ref.shape[1] - w :].astype(F32) * np.float32(256.0)
                    + rim_aux_ref[2:3, rim_aux_ref.shape[1] - w :].astype(F32)
                )
            else:
                pos = pos_ref[0:1, (b - 1) * w : b * w].astype(F32)
            sine, cosine = sin_cos(as_column(pos) * freq_ref[...])
            sine = jnp.where(low, sine, -sine)
            for tile in range(n_kv // 2):
                cols = slice(tile * lanes, (tile + 1) * lanes)
                dk = dk_all[b * w : (b + 1) * w, cols]
                other = jnp.where(low, pltpu.roll(dk, lanes - half, 1), pltpu.roll(dk, half, 1))
                dk_ref[b * w : (b + 1) * w, cols] = (dk * cosine + other * sine).astype(BF16)


def attention_grads(query, grad_out, keys, values, rim, segments, positions, sinks, first):
    rows, width = query.shape
    kv_width = keys.shape[1]
    n_kv = kv_width // HEADDIM
    n_heads = width // HEADDIM
    group = n_heads // n_kv
    w = WINDOW
    lanes = 2 * HEADDIM
    step = group * HEADDIM
    index = np.arange(lanes) % (HEADDIM // 2)
    freq = jnp.asarray((THETA ** (-2.0 * index / HEADDIM)).astype(np.float32)[None, :])
    return pl.pallas_call(
        lambda *refs: attention_kernel(group, n_kv, *refs),
        name="attention_grads",
        grid=(n_kv,),
        in_specs=[
            pl.BlockSpec(memory_space=pltpu.SMEM),
            pl.BlockSpec(memory_space=pltpu.SMEM),
            pl.BlockSpec((rows, step), lambda g: (0, g)),
            pl.BlockSpec((rows, step), lambda g: (0, g)),
            pl.BlockSpec((rows, lanes), lambda g: (0, g // 2)),
            pl.BlockSpec((rows, lanes), lambda g: (0, g // 2)),
            pl.BlockSpec((w, lanes), lambda g: (0, g // 2)),
            pl.BlockSpec((w, lanes), lambda g: (1, g // 2)),
            pl.BlockSpec((16, kv_width), lambda g: (2 * w // 16, 0)),
            pl.BlockSpec((1, rows), lambda g: (0, 0)),
            pl.BlockSpec((1, rows), lambda g: (0, 0)),
            pl.BlockSpec((1, lanes), lambda g: (0, 0)),
        ],
        out_specs=[
            pl.BlockSpec((rows, step), lambda g: (0, g)),
            pl.BlockSpec((rows + w, kv_width), lambda g: (0, 0)),
        ],
        out_shape=[
            jax.ShapeDtypeStruct((rows, width), BF16),
            jax.ShapeDtypeStruct((rows + w, kv_width), BF16),
        ],
        scratch_shapes=[
            pltpu.VMEM((rows + w, lanes), BF16),
            pltpu.VMEM((rows + w, lanes), BF16),
            pltpu.VMEM((HEADDIM, rows + w), BF16),
            pltpu.VMEM((rows // w, w, w), F32),
            pltpu.VMEM((rows + w, lanes), F32),
            pltpu.VMEM((rows + w, kv_width), F32),
        ],
        cost_estimate=pl.CostEstimate(
            flops=10 * rows * 2 * w * width, bytes_accessed=6 * rows * width, transcendentals=rows * w * n_heads
        ),
    )(sinks, first, query, grad_out, keys, values, rim, rim, rim, segments, positions, freq)


def bit_reversed(n):
    bits = n.bit_length() - 1
    return [int(format(i, "b").zfill(bits)[::-1], 2) if bits else 0 for i in range(n)]


def weight_kernel(n_dp, place_ref, inputs_ref, rim_ref, dk_ref, out_ref, scratch):
    rows = inputs_ref.shape[0]
    w = rim_ref.shape[0]
    scratch[...] = dot(inputs_ref[...], dk_ref[w : w + rows, :], 0, 0) + dot(
        rim_ref[...], dk_ref[0:w, :], 0, 0
    )
    piece = scratch.shape[0] // (2 * n_dp)
    for half in range(2):
        for j, relative in enumerate(bit_reversed(n_dp)):
            block = (place_ref[0] ^ relative) * 2 + (place_ref[1] ^ half)
            start = pl.multiple_of(block * piece, piece)
            out_ref[half, j * piece : (j + 1) * piece, :] = scratch[pl.ds(start, piece), :].astype(BF16)


def weight_plain_kernel(inputs_ref, rim_ref, dk_ref, out_ref):
    rows = inputs_ref.shape[0]
    w = rim_ref.shape[0]
    total = dot(inputs_ref[...], dk_ref[w : w + rows, :], 0, 0)
    out_ref[...] = (total + dot(rim_ref[...], dk_ref[0:w, :], 0, 0)).astype(BF16)


def weight_parts(layer_input, rim_input, dk, n_dp, dp_index, core):
    features = layer_input.shape[1]
    kv_width = dk.shape[1]
    piece = features // (2 * n_dp)
    if piece % 16 == 0:
        place = jnp.stack([dp_index, core]).astype(jnp.int32)
        vmem = pl.BlockSpec(memory_space=pltpu.VMEM)
        return pl.pallas_call(
            lambda *refs: weight_kernel(n_dp, *refs),
            name="weight_parts",
            in_specs=[pl.BlockSpec(memory_space=pltpu.SMEM), vmem, vmem, vmem],
            out_specs=vmem,
            out_shape=jax.ShapeDtypeStruct((2, features // 2, kv_width), BF16),
            scratch_shapes=[pltpu.VMEM((features, kv_width), F32)],
            cost_estimate=pl.CostEstimate(
                flops=2 * features * dk.shape[0] * kv_width,
                bytes_accessed=4 * features * kv_width,
                transcendentals=0,
            ),
        )(place, layer_input, rim_input, dk)
    plain = pl.pallas_call(
        weight_plain_kernel,
        name="weight_plain",
        out_shape=jax.ShapeDtypeStruct((features, kv_width), BF16),
    )(layer_input, rim_input, dk)
    plain = plain.reshape(n_dp, 2, piece, kv_width)
    order = jnp.asarray(bit_reversed(n_dp), jnp.int32) ^ dp_index
    plain = jnp.take(plain, order, axis=0)
    halves = [jnp.take(plain, core ^ half, axis=1) for half in range(2)]
    return jnp.stack(halves).reshape(2, features // 2, kv_width)


def exchange(part, axis, by):
    count = lax.axis_size(axis)
    return lax.ppermute(part, axis, [(i, i ^ by) for i in range(count)])


def forward_one(part, axis):
    count = lax.axis_size(axis)
    return lax.ppermute(part, axis, [(i, i + 1) for i in range(count - 1)])


def body(query, keys, values, grad_out, layer_input, sinks, segments, positions):
    rows = query.shape[1]
    w = WINDOW
    n_dp = lax.axis_size("dp")
    n_seq = lax.axis_size("seq")
    dp_index = lax.axis_index("dp")
    seq_index = lax.axis_index("seq")
    core = seq_index % 2

    kv_width = keys.shape[2]
    line = lax.broadcasted_iota(jnp.int32, (16, kv_width), 0)
    seg_row = segments[:, rows - kv_width :]
    pos_row = positions[:, rows - kv_width :]
    aux = jnp.where(line == 0, seg_row, jnp.where(line == 1, pos_row >> 8, pos_row & 255))
    tail = jnp.concatenate([keys[0, rows - w :], values[0, rows - w :], aux.astype(BF16)], axis=0)
    rim = forward_one(tail, "seq")
    rim_input = forward_one(layer_input[0, rows - w :], "seq")

    dq, dk = attention_grads(
        query[0], grad_out[0], keys[0], values[0], rim, segments, positions, sinks, seq_index[None]
    )
    parts = weight_parts(layer_input[0], rim_input, dk, n_dp, dp_index, core)
    total = parts[0].astype(F32) + exchange(parts[1], "seq", 1).astype(F32)
    by = 1
    while by < n_dp:
        half = total.shape[0] // 2
        got = exchange(total[half:].astype(BF16), "dp", by)
        total = total[:half] + got.astype(F32)
        by *= 2
    by = 2
    while by < n_seq:
        mine = total.astype(BF16)
        total = mine.astype(F32) + exchange(mine, "seq", by).astype(F32)
        by *= 2
    other = exchange(total, "seq", 1)
    pair = jnp.where(core == 0, jnp.stack([total, other]), jnp.stack([other, total]))
    return (dq[None], pair.reshape(-1, kv_width))


def solution(mesh):
    return jax.shard_map(
        body,
        mesh=mesh,
        in_specs=(
            P("dp", "seq", None),
            P("dp", "seq", None),
            P("dp", "seq", None),
            P("dp", "seq", None),
            P("dp", "seq", None),
            P(),
            P("dp", "seq"),
            P("dp", "seq"),
        ),
        out_specs=(P("dp", "seq", None), P("dp", None)),
        check_vma=False,
    )
```

time: 174 us -> 58.5 us (0.34)
  waiting for transfers between devices: 92.7 us -> 16.2 us
  matrix products: 20.4 us -> 0 us
  local copies, waits for them, and re-layouts: 22 us -> 4.31 us
  Pallas kernels: 0 us -> 17.4 us
  between operations: 14.5 us -> 0.83 us
  other arithmetic: 13.5 us -> 1.56 us
  starting transfers between devices: 10.2 us -> 17.9 us
    unnamed x3 -> x0, waiting for transfers between devices: 60.4 us -> none
    psum x1 -> x0, waiting for transfers between devices: 30.6 us -> none  [body(): shard = lax.psum(shard, 'seq')]
    dot_general x17 -> x0, matrix products: 20.4 us -> none  [the longest x4 8.07 us: body(): jnp.einsum('qhd,kd->hqk', g_grp, v_grp, preferred_element_type=jnp.float32)]
    pallas_call x0 -> x2, Pallas kernels: none -> 17.4 us  [the longest x1 14.5 us: attention_grads(): pl.pallas_call(lambda *refs: attention_kernel(group, n_kv, *refs), name='...]
    ppermute x4 -> x8, waiting for transfers between devices: 1.64 us -> 16.2 us  [the longest x6 15.8 us: exchange(): return lax.ppermute(part, axis, [(i, i ^ by) for i in range(count)])]
    slice x15 -> x3, local copies, waits for them, and re-layouts: 11.4 us -> 0.04 us  [body(): got = exchange(total[half:].astype(BF16), 'dp', by)]
    ppermute x4 -> x8, starting transfers between devices: 10.1 us -> 17.9 us  [the longest x6 11 us: exchange(): return lax.ppermute(part, axis, [(i, i ^ by) for i in range(count)])]
    convert_element_type x4 -> x2, other arithmetic: 7.44 us -> 0.09 us  [the longest x1 0.07 us: body(): aux.astype(BF16)]
  transfers between devices with their start and end apart: 6 -> 8, of which waited for: 3 -> 7; matrix products, arithmetic and copies ran while one was open for 17% -> 1% of each run, Pallas kernels for 0% -> 25%
where the time goes in v1:
time: 58.5 us; the launch traced here: 58.2 us
  starting transfers between devices  17.9 us (31%)
  Pallas kernels  17.4 us (30%)
  waiting for transfers between devices  16.2 us (28%)
  local copies, waits for them, and re-layouts  4.31 us (7%)
  other arithmetic  1.56 us (3%)
  between operations  0.83 us (1%)
    ppermute x6, waiting for transfers between devices, exchange(): return lax.ppermute(part, axis, [(i, i ^ by) for i in range(count)])  15.8 us
    pallas_call x1, Pallas kernels, attention_grads(): pl.pallas_call(lambda *refs: attention_kernel(group, n_kv, *refs), name='...  14.5 us
    ppermute x6, starting transfers between devices, exchange(): return lax.ppermute(part, axis, [(i, i ^ by) for i in range(count)])  11 us
    ppermute x2, starting transfers between devices, forward_one(): return lax.ppermute(part, axis, [(i, i + 1) for i in range(count - 1)])  6.93 us
    pallas_call x1, Pallas kernels, weight_parts(): pl.pallas_call(lambda *refs: weight_kernel(n_dp, *refs), name='weight_par...  2.87 us
    unnamed x14, local copies, waits for them, and re-layouts  2.1 us
  transfers between devices with their start and end apart: 8, of which 7 were waited for; matrix products, arithmetic and copies ran while one was open for 1% of the time, Pallas kernels for 25%

profile of v1, /device:TPU:0, one launch (start us, length us, event | category | flops | bytes accessed | tf_op | source)
XLA Modules:
  0.0 58.2 jit_solution(12767008646775956190)
XLA Ops:
  0.6 0.0 copy-start.3
  0.6 0.0 copy-start.2
  0.7 1.1 %slice_bitcast_fusion.2 = bf16[128,1536]{1,0:T(8,128)(2,1)S(1)} fusion(bf16[1,256,1536]{2,1,0:T(8,128)(2,1)} %param.13), kind=kLoop, calls=%fused_computation.5 | loop fusion | bytes 786432 | tf_op jit(solution)/shard_map/squeeze | solution.py:300
  1.7 0.0 copy-start.4
  1.7 2.4 %collective-permute-start.1 = (bf16[128,1536]{1,0:T(8,128)(2,1)S(1)}, bf16[128,1536]{1,0:T(8,128)(2,1)S(1)}, u32[]{:S(2)}, u32[]{:S(2)}) collective-permute-start(bf16[128,1536]{1,0:T(8,128)(2,1)S(1)} %slice_bitcast_fusion.2), channel_id=1, source_target_pairs={{0,1},{1,2},{2,3},{4,5},{5,6},{6,7},{8,9},{9,10},{10,11},{12,13},{... | collective-permute-start | bytes 1179656 | tf_op jit(solution)/shard_map/ppermute | solution.py:281
  4.2 0.0 copy-done.4
  4.2 0.0 copy-done.3
  4.2 0.0 copy-done.2
  4.2 0.0 copy-start.5
  4.2 0.7 %copy-done.5 = s32[1,256]{1,0:T(1,128)S(1)} copy-done((s32[1,256]{1,0:T(1,128)S(1)}, s32[1,256]{1,0:T(1,128)}, u32[]{:S(2)}) %copy-start.5) | copy-done | bytes 1048
  4.9 0.1 select_convert_fusion
  5.0 4.5 %collective-permute-start = (bf16[272,256]{1,0:T(8,128)(2,1)S(1)}, bf16[272,256]{1,0:T(8,128)(2,1)S(1)}, u32[]{:S(2)}, u32[]{:S(2)}) collective-permute-start(bf16[272,256]{1,0:T(8,128)(2,1)S(1)} %pad_maximum_fusion), channel_id=1, source_target_pairs={{0,1},{1,2},{2,3},{4,5},{5,6},{6,7},{8,9},{9,10},{10,11},{12,13},{... | collective-permute-start | bytes 417800 | tf_op jit(solution)/shard_map/ppermute | solution.py:281
  9.5 0.6 %pad_add_fusion.refs_0_ = s32[2]{0:T(128)} fusion(s32[1]{0:T(128)} %bitcast.12, s32[1]{0:T(128)} %bitcast.11), kind=kLoop, calls=%fused_computation.17 | loop fusion | flops 2 | bytes 16 | tf_op jit(solution)/shard_map/stack | solution.py:247
  10.2 0.3 collective-permute-done.refs_6_.refs_7_.refs_8_
  10.5 0.0 copy-start.6
  10.5 0.7 %copy-done.6 = bf16[272,256]{1,0:T(8,128)(2,1)} copy-done((bf16[272,256]{1,0:T(8,128)(2,1)}, bf16[272,256]{1,0:T(8,128)(2,1)S(1)}, u32[]{:S(2)}) %copy-start.6) | copy-done | bytes 139288
  11.2 14.5 %attention_grads.1 = (bf16[256,2048]{1,0:T(8,128)(2,1)}, bf16[384,256]{1,0:T(8,128)(2,1)}) custom-call(f32[32]{0:T(128)} %refs_0_.1, s32[1]{0:T(128)} %bitcast.refs_1_, bf16[256,2048]{1,0:T(8,128)(2,1)} %bitcast.37, bf16[256,2048]{1,0:T(8,128)(2,1)} %bitcast.38, bf16[256,256]{1,0:T(8,128)(2,1)} %bitcast.32, bf16[256,256]{1,0:T(8,128)(2,1)} %bitcast.33, ...), custom_call_target="tpu_custom_call" | custom-call | flops 1342177280 | bytes 3145728 | tf_op jit(solution)/shard_map/attention_grads/pallas_call | solution.py:176
  25.7 0.0 collective-permute-done.1.refs_2_
  25.7 0.0 copy-start.1
  25.7 0.7 %copy-done.1 = bf16[128,1536]{1,0:T(8,128)(2,1)} copy-done((bf16[128,1536]{1,0:T(8,128)(2,1)}, bf16[128,1536]{1,0:T(8,128)(2,1)S(1)}, u32[]{:S(2)}) %copy-start.1) | copy-done | bytes 393240
  26.4 2.9 %weight_parts.1 = bf16[2,768,256]{2,1,0:T(8,128)(2,1)} custom-call(s32[2]{0:T(128)} %pad_add_fusion.refs_0_, bf16[256,1536]{1,0:T(8,128)(2,1)} %bitcast.29, bf16[128,1536]{1,0:T(8,128)(2,1)} %copy-done.1, bf16[384,256]{1,0:T(8,128)(2,1)} %get-tuple-element.5.refs_3_), custom_call_target="tpu_custom_call" | custom-call | flops 301989888 | bytes 1572864 | tf_op jit(solution)/shard_map/weight_parts/pallas_call | solution.py:249
  29.3 0.0 copy-start
  29.3 1.1 %slice_bitcast_fusion = bf16[768,256]{1,0:T(8,128)(2,1)S(1)} fusion(bf16[2,768,256]{2,1,0:T(8,128)(2,1)} %weight_parts.1), kind=kLoop, calls=%fused_computation.3 | loop fusion | bytes 786432 | tf_op jit(solution)/shard_map/squeeze | solution.py:306
  30.4 2.5 %collective-permute-start.2 = (bf16[768,256]{1,0:T(8,128)(2,1)S(1)}, bf16[768,256]{1,0:T(8,128)(2,1)S(1)}, u32[]{:S(2)}, u32[]{:S(2)}) collective-permute-start(bf16[768,256]{1,0:T(8,128)(2,1)S(1)} %slice_bitcast_fusion), channel_id=1, source_target_pairs={{0,1},{1,0},{2,3},{3,2},{4,5},{5,4},{6,7},{7,6},{8,9},{9,8},{10,11... | collective-permute-start | bytes 1179656 | tf_op jit(solution)/shard_map/ppermute | solution.py:276
  32.9 1.3 %collective-permute-done.2 = bf16[768,256]{1,0:T(8,128)(2,1)S(1)} collective-permute-done((bf16[768,256]{1,0:T(8,128)(2,1)S(1)}, bf16[768,256]{1,0:T(8,128)(2,1)S(1)}, u32[]{:S(2)}, u32[]{:S(2)}) %collective-permute-start.2) | collective-permute-done | bytes 393248 | tf_op jit(solution)/shard_map/ppermute | solution.py:276
  34.3 0.0 copy-done
  34.3 0.1 convert_add_fusion
  34.4 1.6 %collective-permute-start.3 = (bf16[384,256]{1,0:T(8,128)(2,1)S(1)}, bf16[384,256]{1,0:T(8,128)(2,1)S(1)}, u32[]{:S(2)}, u32[]{:S(2)}) collective-permute-start(bf16[384,256]{1,0:T(8,128)(2,1)S(1)} %slice.70), channel_id=1, source_target_pairs={{0,4},{4,0},{8,12},{12,8},{16,20},{20,16},{24,28},{28,24},{1,5},{5... | collective-permute-start | bytes 589832 | tf_op jit(solution)/shard_map/ppermute | solution.py:276
  36.0 5.7 %collective-permute-done.3 = bf16[384,256]{1,0:T(8,128)(2,1)S(1)} collective-permute-done((bf16[384,256]{1,0:T(8,128)(2,1)S(1)}, bf16[384,256]{1,0:T(8,128)(2,1)S(1)}, u32[]{:S(2)}, u32[]{:S(2)}) %collective-permute-start.3) | collective-permute-done | bytes 196640 | tf_op jit(solution)/shard_map/ppermute | solution.py:276
  41.7 1.6 %collective-permute-start.4 = (bf16[192,256]{1,0:T(8,128)(2,1)S(1)}, bf16[192,256]{1,0:T(8,128)(2,1)S(1)}, u32[]{:S(2)}, u32[]{:S(2)}) collective-permute-start(bf16[192,256]{1,0:T(8,128)(2,1)S(1)} %slice.71), channel_id=1, source_target_pairs={{0,8},{4,12},{8,0},{12,4},{16,24},{20,28},{24,16},{28,20},{1,9},{5... | collective-permute-start | bytes 294920 | tf_op jit(solution)/shard_map/ppermute | solution.py:276
  43.3 3.0 %collective-permute-done.4 = bf16[192,256]{1,0:T(8,128)(2,1)S(1)} collective-permute-done((bf16[192,256]{1,0:T(8,128)(2,1)S(1)}, bf16[192,256]{1,0:T(8,128)(2,1)S(1)}, u32[]{:S(2)}, u32[]{:S(2)}) %collective-permute-start.4) | collective-permute-done | bytes 98336 | tf_op jit(solution)/shard_map/ppermute | solution.py:276
  46.4 2.7 %collective-permute-start.5 = (bf16[96,256]{1,0:T(8,128)(2,1)S(1)}, bf16[96,256]{1,0:T(8,128)(2,1)S(1)}, u32[]{:S(2)}, u32[]{:S(2)}) collective-permute-start(bf16[96,256]{1,0:T(8,128)(2,1)S(1)} %slice.72), channel_id=1, source_target_pairs={{0,16},{4,20},{8,24},{12,28},{16,0},{20,4},{24,8},{28,12},{1,17},{... | collective-permute-start | bytes 147464 | tf_op jit(solution)/shard_map/ppermute | solution.py:276
  49.1 2.4 %collective-permute-done.5 = bf16[96,256]{1,0:T(8,128)(2,1)S(1)} collective-permute-done((bf16[96,256]{1,0:T(8,128)(2,1)S(1)}, bf16[96,256]{1,0:T(8,128)(2,1)S(1)}, u32[]{:S(2)}, u32[]{:S(2)}) %collective-permute-start.5) | collective-permute-done | bytes 49184 | tf_op jit(solution)/shard_map/ppermute | solution.py:276
  51.5 2.6 %collective-permute-start.6 = (bf16[96,256]{1,0:T(8,128)(2,1)S(1)}, bf16[96,256]{1,0:T(8,128)(2,1)S(1)}, u32[]{:S(2)}, u32[]{:S(2)}) collective-permute-start(bf16[96,256]{1,0:T(8,128)(2,1)S(1)} %fusion), channel_id=1, source_target_pairs={{0,2},{1,3},{2,0},{3,1},{4,6},{5,7},{6,4},{7,5},{8,10},{9,11},{10,... | collective-permute-start | bytes 147464 | tf_op jit(solution)/shard_map/ppermute | solution.py:276
  54.1 2.1 %collective-permute-done.6 = bf16[96,256]{1,0:T(8,128)(2,1)S(1)} collective-permute-done((bf16[96,256]{1,0:T(8,128)(2,1)S(1)}, bf16[96,256]{1,0:T(8,128)(2,1)S(1)}, u32[]{:S(2)}, u32[]{:S(2)}) %collective-permute-start.6) | collective-permute-done | bytes 49184 | tf_op jit(solution)/shard_map/ppermute | solution.py:276
  56.1 0.1 collective-permute-start.7
  56.2 1.3 %collective-permute-done.7 = f32[96,256]{1,0:T(8,128)S(1)} collective-permute-done((f32[96,256]{1,0:T(8,128)S(1)}, f32[96,256]{1,0:T(8,128)S(1)}, u32[]{:S(2)}, u32[]{:S(2)}) %collective-permute-start.7) | collective-permute-done | bytes 98336 | tf_op jit(solution)/shard_map/ppermute | solution.py:276
  57.5 0.7 %maximum_select_fusion = f32[2,96,256]{2,1,0:T(8,128)} fusion(f32[1,96,256]{2,1,0:T(8,128)S(1)} %bitcast.31, f32[1,96,256]{2,1,0:T(8,128)S(1)} %get-tuple-element.6, pred[]{:T(512)S(6)} %eq.23), kind=kLoop, calls=%fused_computation.8 | loop fusion | flops 147456 | bytes 393217 | tf_op jit(solution)/shard_map/jit(_where)/select_n | solution.py:319
  (11 shorter events, 0.2 us)
Async XLA Ops:
  0.6 3.6 %copy-start.3 = (bf16[1,256,256]{2,1,0:T(8,128)(2,1)S(1)}, bf16[1,256,256]{2,1,0:T(8,128)(2,1)}, u32[]{:S(2)}) copy-start(bf16[1,256,256]{2,1,0:T(8,128)(2,1)} %param.11) | copy-start | bytes 393220
  0.6 3.6 %copy-start.2 = (bf16[1,256,256]{2,1,0:T(8,128)(2,1)S(1)}, bf16[1,256,256]{2,1,0:T(8,128)(2,1)}, u32[]{:S(2)}) copy-start(bf16[1,256,256]{2,1,0:T(8,128)(2,1)} %param.10) | copy-start | bytes 393220
  1.7 2.5 %copy-start.4 = (s32[1,256]{1,0:T(1,128)S(1)}, s32[1,256]{1,0:T(1,128)}, u32[]{:S(2)}) copy-start(s32[1,256]{1,0:T(1,128)} %refs_10_.1) | copy-start | bytes 3076
  1.7 23.9 %collective-permute-start.1 = (bf16[128,1536]{1,0:T(8,128)(2,1)S(1)}, bf16[128,1536]{1,0:T(8,128)(2,1)S(1)}, u32[]{:S(2)}, u32[]{:S(2)}) collective-permute-start(bf16[128,1536]{1,0:T(8,128)(2,1)S(1)} %slice_bitcast_fusion.2), channel_id=1, source_target_pairs={{0,1},{1,2},{2,3},{4,5},{5,6},{6,7},{8,9},{9,10},{10,11},{12,13},{... | collective-permute-start | bytes 1179656 | tf_op jit(solution)/shard_map/ppermute | solution.py:281
  4.2 0.7 %copy-start.5 = (s32[1,256]{1,0:T(1,128)S(1)}, s32[1,256]{1,0:T(1,128)}, u32[]{:S(2)}) copy-start(s32[1,256]{1,0:T(1,128)} %refs_9_.1) | copy-start | bytes 3076
  5.0 5.5 %collective-permute-start = (bf16[272,256]{1,0:T(8,128)(2,1)S(1)}, bf16[272,256]{1,0:T(8,128)(2,1)S(1)}, u32[]{:S(2)}, u32[]{:S(2)}) collective-permute-start(bf16[272,256]{1,0:T(8,128)(2,1)S(1)} %pad_maximum_fusion), channel_id=1, source_target_pairs={{0,1},{1,2},{2,3},{4,5},{5,6},{6,7},{8,9},{9,10},{10,11},{12,13},{... | collective-permute-start | bytes 417800 | tf_op jit(solution)/shard_map/ppermute | solution.py:281
  10.5 0.7 %copy-start.6 = (bf16[272,256]{1,0:T(8,128)(2,1)}, bf16[272,256]{1,0:T(8,128)(2,1)S(1)}, u32[]{:S(2)}) copy-start(bf16[272,256]{1,0:T(8,128)(2,1)S(1)} %collective-permute-done.refs_6_.refs_7_.refs_8_) | copy-start | bytes 417796
  25.7 0.8 %copy-start.1 = (bf16[128,1536]{1,0:T(8,128)(2,1)}, bf16[128,1536]{1,0:T(8,128)(2,1)S(1)}, u32[]{:S(2)}) copy-start(bf16[128,1536]{1,0:T(8,128)(2,1)S(1)} %collective-permute-done.1.refs_2_) | copy-start | bytes 1179652
  29.3 5.0 %copy-start = (bf16[2,768,256]{2,1,0:T(8,128)(2,1)S(1)}, bf16[2,768,256]{2,1,0:T(8,128)(2,1)}, u32[]{:S(2)}) copy-start(bf16[2,768,256]{2,1,0:T(8,128)(2,1)} %weight_parts.1) | copy-start | bytes 2359300
  30.4 3.9 %collective-permute-start.2 = (bf16[768,256]{1,0:T(8,128)(2,1)S(1)}, bf16[768,256]{1,0:T(8,128)(2,1)S(1)}, u32[]{:S(2)}, u32[]{:S(2)}) collective-permute-start(bf16[768,256]{1,0:T(8,128)(2,1)S(1)} %slice_bitcast_fusion), channel_id=1, source_target_pairs={{0,1},{1,0},{2,3},{3,2},{4,5},{5,4},{6,7},{7,6},{8,9},{9,8},{10,11... | collective-permute-start | bytes 1179656 | tf_op jit(solution)/shard_map/ppermute | solution.py:276
  34.4 7.2 %collective-permute-start.3 = (bf16[384,256]{1,0:T(8,128)(2,1)S(1)}, bf16[384,256]{1,0:T(8,128)(2,1)S(1)}, u32[]{:S(2)}, u32[]{:S(2)}) collective-permute-start(bf16[384,256]{1,0:T(8,128)(2,1)S(1)} %slice.70), channel_id=1, source_target_pairs={{0,4},{4,0},{8,12},{12,8},{16,20},{20,16},{24,28},{28,24},{1,5},{5... | collective-permute-start | bytes 589832 | tf_op jit(solution)/shard_map/ppermute | solution.py:276
  41.7 4.7 %collective-permute-start.4 = (bf16[192,256]{1,0:T(8,128)(2,1)S(1)}, bf16[192,256]{1,0:T(8,128)(2,1)S(1)}, u32[]{:S(2)}, u32[]{:S(2)}) collective-permute-start(bf16[192,256]{1,0:T(8,128)(2,1)S(1)} %slice.71), channel_id=1, source_target_pairs={{0,8},{4,12},{8,0},{12,4},{16,24},{20,28},{24,16},{28,20},{1,9},{5... | collective-permute-start | bytes 294920 | tf_op jit(solution)/shard_map/ppermute | solution.py:276
  46.4 5.1 %collective-permute-start.5 = (bf16[96,256]{1,0:T(8,128)(2,1)S(1)}, bf16[96,256]{1,0:T(8,128)(2,1)S(1)}, u32[]{:S(2)}, u32[]{:S(2)}) collective-permute-start(bf16[96,256]{1,0:T(8,128)(2,1)S(1)} %slice.72), channel_id=1, source_target_pairs={{0,16},{4,20},{8,24},{12,28},{16,0},{20,4},{24,8},{28,12},{1,17},{... | collective-permute-start | bytes 147464 | tf_op jit(solution)/shard_map/ppermute | solution.py:276
  51.5 4.6 %collective-permute-start.6 = (bf16[96,256]{1,0:T(8,128)(2,1)S(1)}, bf16[96,256]{1,0:T(8,128)(2,1)S(1)}, u32[]{:S(2)}, u32[]{:S(2)}) collective-permute-start(bf16[96,256]{1,0:T(8,128)(2,1)S(1)} %fusion), channel_id=1, source_target_pairs={{0,2},{1,3},{2,0},{3,1},{4,6},{5,7},{6,4},{7,5},{8,10},{9,11},{10,... | collective-permute-start | bytes 147464 | tf_op jit(solution)/shard_map/ppermute | solution.py:276
  56.1 1.4 %collective-permute-start.7 = (f32[96,256]{1,0:T(8,128)S(1)}, f32[96,256]{1,0:T(8,128)S(1)}, u32[]{:S(2)}, u32[]{:S(2)}) collective-permute-start(f32[96,256]{1,0:T(8,128)S(1)} %get-tuple-element.7), channel_id=1, source_target_pairs={{0,1},{1,0},{2,3},{3,2},{4,5},{5,4},{6,7},{7,6},{8,9},{9,8},{10,11... | collective-permute-start | bytes 294920 | tf_op jit(solution)/shard_map/ppermute | solution.py:276

commit v2 on v0

v2 whole, which is shorter than its diff:
```python
import jax
import jax.numpy as jnp
import numpy as np
from jax import lax
from jax.experimental import pallas as pl
from jax.experimental.pallas import tpu as pltpu
from jax.sharding import PartitionSpec as P

HEADDIM = 64
WINDOW = 128
THETA = 150000.0
LOW = -1e30

F32 = jnp.float32
BF16 = jnp.bfloat16


def dot(a, b, ca, cb):
    return lax.dot_general(a, b, (((ca,), (cb,)), ((), ())), preferred_element_type=F32)


def iota(shape, dim):
    return lax.broadcasted_iota(jnp.int32, shape, dim)


def sin_cos(angle):
    turns = jnp.floor(angle * np.float32(2.0 / np.pi) + np.float32(0.5))
    rest = angle - turns * np.float32(1.5703125)
    rest = rest - turns * np.float32(4.837512969970703125e-4)
    rest = rest - turns * np.float32(7.54978995489188216e-8)
    sq = rest * rest
    sin_part = np.float32(-1.9515295891e-4) * sq + np.float32(8.3321608736e-3)
    sin_part = (sin_part * sq + np.float32(-1.6666654611e-1)) * sq * rest + rest
    cos_part = np.float32(2.443315711809948e-5) * sq + np.float32(-1.388731625493765e-3)
    cos_part = (cos_part * sq + np.float32(4.166664568298827e-2)) * sq * sq
    cos_part = cos_part - np.float32(0.5) * sq + np.float32(1.0)
    quadrant = turns.astype(jnp.int32)
    odd = (quadrant & 1) == 1
    sine = jnp.where(odd, cos_part, sin_part)
    cosine = jnp.where(odd, sin_part, cos_part)
    sine = jnp.where((quadrant & 2) == 2, -sine, sine)
    cosine = jnp.where(((quadrant + 1) & 2) == 2, -cosine, cosine)
    return sine, cosine


def as_column(row):
    return jnp.broadcast_to(row, (row.shape[1], row.shape[1])).T


def load(copies):
    for copy in copies:
        copy.start()
    return copies


def prepare_keys(kv, blocks, keys2, values2, keys_t):
    w = WINDOW
    lanes = 2 * HEADDIM
    own_half = (iota((w, lanes), 1) < HEADDIM) == (kv % 2 == 0)
    cols = slice(kv // 2 * lanes, (kv // 2 + 1) * lanes)
    for b, (k_ref, v_ref, first_row) in enumerate(blocks):
        k_tile = k_ref[first_row : first_row + w, cols].astype(F32) * np.float32(HEADDIM**-0.5)
        v_tile = v_ref[first_row : first_row + w, cols].astype(F32)
        k_tile = jnp.where(own_half, k_tile, pltpu.roll(k_tile, HEADDIM, 1))
        v_tile = jnp.where(own_half, v_tile, pltpu.roll(v_tile, HEADDIM, 1))
        keys2[kv, b * w : (b + 1) * w, :] = k_tile.astype(BF16)
        values2[kv, b * w : (b + 1) * w, :] = v_tile.astype(BF16)
        keys_t[kv, :, b * w : (b + 1) * w] = k_tile.T[:HEADDIM].astype(BF16)


def attend(n_kv, group, row_blocks, wait_kv, done_kv, sinks_ref, query, grad, dq, bias, scratch, add_dk):
    keys2, values2, keys_t, scores_s, grads_s, q2_s, ds_s = scratch
    w = WINDOW
    lanes = 2 * HEADDIM
    pairs = group // 2
    lower = iota((w, lanes), 1) < HEADDIM
    tri = iota((w, w), 0) <= iota((w, w), 1)
    tri2 = jnp.concatenate([tri, tri], axis=1)
    zero = jnp.zeros((), BF16)
    items = [(b, kv, pair) for kv in range(n_kv) for b in range(row_blocks) for pair in range(pairs)]

    def to_scores(n):
        b, kv, pair = items[n]
        if b == 0 and pair == 0:
            wait_kv(kv)
        unit = (n // pairs) % 2
        rows = slice(b * w, (b + 1) * w)
        cols = slice((kv * pairs + pair) * lanes, (kv * pairs + pair + 1) * lanes)
        window = slice(b * w, (b + 2) * w)
        q_tile = query[rows, cols]
        g_tile = grad[rows, cols]
        q2 = jnp.concatenate([jnp.where(lower, q_tile, zero), jnp.where(lower, zero, q_tile)], 0)
        g2 = jnp.concatenate([jnp.where(lower, g_tile, zero), jnp.where(lower, zero, g_tile)], 0)
        q2_s[unit, pair * 2 * w : (pair + 1) * 2 * w, :] = q2
        scores = dot(keys2[kv, window, :], q2, 1, 1)
        bias2 = jnp.concatenate([bias[b], bias[b]], axis=1)
        scores_s[n % 2] = jnp.where(tri2, scores[w:], scores[:w]) + bias2
        grads = dot(values2[kv, window, :], g2, 1, 1)
        grads_s[n % 2] = jnp.where(tri2, grads[w:], grads[:w])

    def to_ds(n):
        b, kv, pair = items[n]
        unit = (n // pairs) % 2
        for one in range(2):
            cols = slice(one * w, (one + 1) * w)
            sink = sinks_ref[kv * group + 2 * pair + one]
            scores = scores_s[n % 2, :, cols]
            peak = jnp.maximum(jnp.max(scores, axis=0, keepdims=True), sink)
            expo = jnp.exp(scores - peak)
            total = jnp.sum(expo, axis=0, keepdims=True) + jnp.exp(sink - peak)
            probs = expo * (np.float32(1.0) / total)
            grads = grads_s[n % 2, :, cols]
            delta = jnp.sum(probs * grads, axis=0, keepdims=True)
            ds = probs * (grads - delta)
            out_cols = slice(pair * 2 * w + one * w, pair * 2 * w + (one + 1) * w)
            ds_s[unit, 0:w, out_cols] = jnp.where(tri, np.float32(0.0), ds).astype(BF16)
            ds_s[unit, w : 2 * w, out_cols] = jnp.where(tri, ds, np.float32(0.0)).astype(BF16)

    def to_grads(n):
        b, kv, pair = items[n]
        unit = (n // pairs) % 2
        rows = slice(b * w, (b + 1) * w)
        cols = slice((kv * pairs + pair) * lanes, (kv * pairs + pair + 1) * lanes)
        ds = ds_s[unit, :, pair * 2 * w : (pair + 1) * 2 * w]
        dq_t = dot(keys_t[kv, :, b * w : (b + 2) * w], ds, 1, 0)
        dq_t = jnp.concatenate([dq_t[:, :w], dq_t[:, w:]], axis=0)
        dq[rows, cols] = dq_t.T.astype(BF16)
        if pair == pairs - 1:
            add_dk(b, kv, dot(ds_s[unit], q2_s[unit], 1, 0))
            if b == row_blocks - 1:
                done_kv(kv)

    for n in range(len(items) + 2):
        if n < len(items):
            to_scores(n)
        if 0 <= n - 1 < len(items):
            to_ds(n - 1)
        if n >= 2:
            to_grads(n - 2)


def attend_scratch(n_kv, group, row_blocks):
    w = WINDOW
    lanes = 2 * HEADDIM
    return [
        pltpu.VMEM((n_kv, (row_blocks + 1) * w, lanes), BF16),
        pltpu.VMEM((n_kv, (row_blocks + 1) * w, lanes), BF16),
        pltpu.VMEM((n_kv, HEADDIM, (row_blocks + 1) * w), BF16),
        pltpu.VMEM((2, w, 2 * w), F32),
        pltpu.VMEM((2, w, 2 * w), F32),
        pltpu.VMEM((2, group * w, lanes), BF16),
        pltpu.VMEM((2, 2 * w, group * w), BF16),
    ]


def window_bias(bias, b, prev_segs, own_segs):
    tri = iota((WINDOW, WINDOW), 0) <= iota((WINDOW, WINDOW), 1)
    key_segs = jnp.where(tri, as_column(own_segs), as_column(prev_segs))
    bias[b] = jnp.where(key_segs == own_segs, np.float32(0.0), np.float32(LOW))


def store_dk(dk_part, dk_all, first_block, b, kv, part, seen):
    w = WINDOW
    lanes = 2 * HEADDIM
    if kv % 2 == 0:
        dk_part[b] = part
        return
    even = dk_part[b]
    low = iota(part.shape, 1) < HEADDIM
    both = jnp.where(low, even, part) + pltpu.roll(jnp.where(low, part, even), HEADDIM, 1)
    cols = slice(kv // 2 * lanes, (kv // 2 + 1) * lanes)
    for k in range(2):
        rows = slice((first_block + b + k) * w, (first_block + b + k + 1) * w)
        piece = both[k * w : (k + 1) * w]
        if (first_block + b + k, kv) in seen:
            piece = piece + dk_all[rows, cols]
        seen.add((first_block + b + k, kv))
        dk_all[rows, cols] = piece


def rotate(dk, sine, cosine):
    half = HEADDIM // 2
    lanes = dk.shape[1]
    low = (iota(dk.shape, 1) % HEADDIM) < half
    other = jnp.where(low, pltpu.roll(dk, lanes - half, 1), pltpu.roll(dk, half, 1))
    return (dk * cosine + other * sine) * np.float32(HEADDIM**-0.5)


def turn_table(pos, freq):
    sine, cosine = sin_cos(as_column(pos.astype(F32)) * freq)
    low = (iota(sine.shape, 1) % HEADDIM) < HEADDIM // 2
    return jnp.where(low, sine, -sine), cosine


def local_kernel(
    n_kv, group, sinks_ref, segs_ref, pos_ref, freq_ref, query_hbm, grad_hbm, keys_hbm, values_hbm,
    dq_hbm, dk_ref, own_ref, table_ref,
    query, grad, dq, keys, values, bias, dk_part, dk_all, key_sem, in_sem, out_sem, *scratch,
):
    w = WINDOW
    lanes = 2 * HEADDIM
    rows = keys.shape[0]
    row_blocks = rows // w - 1
    step = group * HEADDIM
    key_copies = load(
        [
            pltpu.make_async_copy(keys_hbm, keys, key_sem.at[0]),
            pltpu.make_async_copy(values_hbm, values, key_sem.at[1]),
        ]
    )

    def ins(kv):
        cols = slice(kv * step, (kv + 1) * step)
        return [
            pltpu.make_async_copy(query_hbm.at[w:, cols], query.at[:, cols], in_sem.at[0, kv]),
            pltpu.make_async_copy(grad_hbm.at[w:, cols], grad.at[:, cols], in_sem.at[1, kv]),
        ]

    def out(kv):
        cols = slice(kv * step, (kv + 1) * step)
        return pltpu.make_async_copy(dq.at[:, cols], dq_hbm.at[w:, cols], out_sem.at[kv])

    in_copies = [load(ins(kv)) for kv in range(n_kv)]
    segs = [segs_ref[0:1, b * w : (b + 1) * w].astype(F32) for b in range(row_blocks + 1)]
    for b in range(row_blocks):
        window_bias(bias, b, segs[b], segs[b + 1])
    tables = []
    for b in range(row_blocks + 1):
        sine, cosine = turn_table(pos_ref[0:1, b * w : (b + 1) * w], freq_ref[...])
        table_ref[2 * b] = sine
        table_ref[2 * b + 1] = cosine
    for copy in key_copies:
        copy.wait()
    seen = set()

    def wait_kv(kv):
        prepare_keys(kv, [(keys, values, b * w) for b in range(row_blocks + 1)], *scratch[:3])
        for copy in in_copies[kv]:
            copy.wait()

    attend(
        n_kv, group, row_blocks, wait_kv, lambda kv: out(kv).start(), sinks_ref, query, grad, dq, bias, scratch,
        lambda b, kv, part: store_dk(dk_part, dk_all, 0, b, kv, part, seen),
    )
    for b in range(row_blocks + 1):
        for tile in range(n_kv // 2):
            cols = slice(tile * lanes, (tile + 1) * lanes)
            turned = rotate(dk_all[b * w : (b + 1) * w, cols], table_ref[2 * b], table_ref[2 * b + 1])
            if b == 0:
                own_ref[:, cols] = turned
            else:
                dk_ref[(b - 1) * w : b * w, cols] = turned.astype(BF16)
    for kv in range(n_kv):
        out(kv).wait()


def rim_kernel(
    n_kv, group, n_dp, place_ref, sinks_ref, segs_ref, freq_ref, dk_ref, own_ref, table_ref,
    query_hbm, grad_hbm, keys_hbm, values_hbm, inputs_hbm, rim_hbm, dq_in,
    dq_hbm, send_ref, keep_ref,
    query, grad, dq, keys, values, inputs, rim, bias, dk_part, dk_all, dk16, sums, key_sem, in_sem, out_sem,
    *scratch,
):
    w = WINDOW
    lanes = 2 * HEADDIM
    step = group * HEADDIM
    features = inputs.shape[1]
    kv_width = n_kv * HEADDIM
    rows = inputs.shape[0]
    key_copies = load(
        [
            pltpu.make_async_copy(keys_hbm.at[0:w], keys, key_sem.at[0]),
            pltpu.make_async_copy(values_hbm.at[0:w], values, key_sem.at[1]),
            pltpu.make_async_copy(rim_hbm, rim, key_sem.at[2]),
        ]
    )

    def ins(kv):
        cols = slice(kv * step, (kv + 1) * step)
        return [
            pltpu.make_async_copy(query_hbm.at[0:w, cols], query.at[:, cols], in_sem.at[0, kv]),
            pltpu.make_async_copy(grad_hbm.at[0:w, cols], grad.at[:, cols], in_sem.at[1, kv]),
        ]

    def out(kv):
        cols = slice(kv * step, (kv + 1) * step)
        return pltpu.make_async_copy(dq.at[:, cols], dq_hbm.at[0:w, cols], out_sem.at[kv])

    in_copies = [load(ins(kv)) for kv in range(n_kv)]
    inputs_copy = pltpu.make_async_copy(inputs_hbm, inputs, key_sem.at[3])
    inputs_copy.start()
    for copy in key_copies:
        copy.wait()
    rim_keys = rim.at[:, features : features + kv_width]
    rim_values = rim.at[:, features + kv_width : features + 2 * kv_width]
    aux = rim[0:16, features + 2 * kv_width :].astype(F32)
    rim_segs = jnp.where(place_ref[2] == 0, np.float32(-1.0), aux[0:1])
    window_bias(bias, 0, rim_segs, segs_ref[0:1, 0:w].astype(F32))
    rim_sine, rim_cosine = turn_table(aux[1:2] * np.float32(256.0) + aux[2:3], freq_ref[...])
    seen = set()

    def wait_kv(kv):
        prepare_keys(kv, [(rim_keys, rim_values, 0), (keys, values, 0)], *scratch[:3])
        for copy in in_copies[kv]:
            copy.wait()

    attend(
        n_kv, group, 1, wait_kv, lambda kv: out(kv).start(), sinks_ref, query, grad, dq, bias, scratch,
        lambda b, kv, part: store_dk(dk_part, dk_all, 0, b, kv, part, seen),
    )
    for tile in range(n_kv // 2):
        cols = slice(tile * lanes, (tile + 1) * lanes)
        dk16[0:w, cols] = rotate(dk_all[0:w, cols], rim_sine, rim_cosine).astype(BF16)
        own = rotate(dk_all[w : 2 * w, cols], table_ref[0], table_ref[1]) + own_ref[:, cols]
        dk16[w : 2 * w, cols] = own.astype(BF16)
    if rows > w:
        dk16[2 * w :, :] = dk_ref[...]
    inputs_copy.wait()
    sums[...] = dot(inputs[...], dk16[w:, :], 0, 0) + dot(rim[:, 0:features], dk16[0:w, :], 0, 0)
    piece = features // (2 * n_dp)
    for half, ref in enumerate([keep_ref, send_ref]):
        for j, relative in enumerate(bit_reversed(n_dp)):
            if piece % 16 == 0:
                block = (place_ref[0] ^ relative) * 2 + (place_ref[1] ^ half)
                start = pl.multiple_of(block * piece, piece)
                ref[j * piece : (j + 1) * piece, :] = sums[pl.ds(start, piece), :].astype(BF16)
    if piece % 16:
        keep_ref[...] = sums[0 : features // 2, :].astype(BF16)
        send_ref[...] = sums[features // 2 :, :].astype(BF16)
    for kv in range(n_kv):
        out(kv).wait()


ANY = pl.BlockSpec(memory_space=pl.ANY)
HBM = pl.BlockSpec(memory_space=pltpu.HBM)
VMEM = pl.BlockSpec(memory_space=pltpu.VMEM)
SMEM = pl.BlockSpec(memory_space=pltpu.SMEM)
LIMIT = 24 * 2**20


def rotation_rates():
    index = np.arange(2 * HEADDIM) % (HEADDIM // 2)
    return jnp.asarray((THETA ** (-2.0 * index / HEADDIM)).astype(np.float32)[None, :])


def shared_scratch(n_kv, group, row_blocks):
    w = WINDOW
    width = n_kv * group * HEADDIM
    lanes = 2 * HEADDIM
    wide = pltpu.VMEM((row_blocks * w, width), BF16)
    return [wide, wide, wide]


def estimate(row_blocks, width, extra_flops, extra_bytes):
    w = WINDOW
    return pl.CostEstimate(
        flops=10 * row_blocks * w * 2 * w * width + extra_flops,
        bytes_accessed=6 * row_blocks * w * width + extra_bytes,
        transcendentals=row_blocks * w * w * width // HEADDIM,
    )


def local_grads(query, grad_out, keys, values, segments, positions, sinks):
    rows, width = query.shape
    kv_width = keys.shape[1]
    n_kv = kv_width // HEADDIM
    group = width // kv_width
    w = WINDOW
    lanes = 2 * HEADDIM
    row_blocks = rows // w - 1
    return pl.pallas_call(
        lambda *refs: local_kernel(n_kv, group, *refs),
        name="local_grads",
        in_specs=[SMEM, VMEM, VMEM, VMEM, HBM, HBM, HBM, HBM],
        out_specs=[HBM, VMEM, VMEM, VMEM],
        out_shape=[
            jax.ShapeDtypeStruct((rows, width), BF16),
            jax.ShapeDtypeStruct((rows - w, kv_width), BF16),
            jax.ShapeDtypeStruct((w, kv_width), F32),
            jax.ShapeDtypeStruct((2 * (row_blocks + 1), w, lanes), F32),
        ],
        scratch_shapes=shared_scratch(n_kv, group, row_blocks)
        + [
            pltpu.VMEM((rows, kv_width), BF16),
            pltpu.VMEM((rows, kv_width), BF16),
            pltpu.VMEM((row_blocks, w, w), F32),
            pltpu.VMEM((row_blocks, 2 * w, lanes), F32),
            pltpu.VMEM((rows, kv_width), F32),
            pltpu.SemaphoreType.DMA((2,)),
            pltpu.SemaphoreType.DMA((2, n_kv)),
            pltpu.SemaphoreType.DMA((n_kv,)),
        ]
        + attend_scratch(n_kv, group, row_blocks),
        compiler_params=pltpu.CompilerParams(vmem_limit_bytes=LIMIT),
        cost_estimate=estimate(row_blocks, width, 0, 0),
    )(sinks, segments, positions, rotation_rates(), query, grad_out, keys, values)


def rim_grads(local, query, grad_out, keys, values, layer_input, rim, segments, sinks, place, n_dp):
    dq, dk, own, table = local
    rows, width = query.shape
    kv_width = keys.shape[1]
    features = layer_input.shape[1]
    n_kv = kv_width // HEADDIM
    group = width // kv_width
    w = WINDOW
    lanes = 2 * HEADDIM
    return pl.pallas_call(
        lambda *refs: rim_kernel(n_kv, group, n_dp, *refs),
        name="rim_grads",
        in_specs=[SMEM, SMEM] + [VMEM] * 5 + [HBM] * 5 + [ANY, HBM],
        out_specs=[HBM, VMEM, VMEM],
        out_shape=[
            jax.ShapeDtypeStruct((rows, width), BF16),
            jax.ShapeDtypeStruct((features // 2, kv_width), BF16),
            jax.ShapeDtypeStruct((features // 2, kv_width), BF16),
        ],
        input_output_aliases={13: 0},
        scratch_shapes=shared_scratch(n_kv, group, 1)
        + [
            pltpu.VMEM((w, kv_width), BF16),
            pltpu.VMEM((w, kv_width), BF16),
            pltpu.VMEM((rows, features), BF16),
            pltpu.VMEM(rim.shape, BF16),
            pltpu.VMEM((1, w, w), F32),
            pltpu.VMEM((1, 2 * w, lanes), F32),
            pltpu.VMEM((2 * w, kv_width), F32),
            pltpu.VMEM((rows + w, kv_width), BF16),
            pltpu.VMEM((features, kv_width), F32),
            pltpu.SemaphoreType.DMA((4,)),
            pltpu.SemaphoreType.DMA((2, n_kv)),
            pltpu.SemaphoreType.DMA((n_kv,)),
        ]
        + attend_scratch(n_kv, group, 1),
        compiler_params=pltpu.CompilerParams(vmem_limit_bytes=LIMIT),
        cost_estimate=estimate(1, width, 2 * features * kv_width * (rows + w), 8 * features * kv_width),
    )(place, sinks, segments, rotation_rates(), dk, own, table, query, grad_out, keys, values, layer_input, rim, dq)


def tail_kernel(segs_ref, pos_ref, inputs_hbm, keys_hbm, values_hbm, out_ref, sem):
    w = WINDOW
    rows, features = inputs_hbm.shape
    kv_width = keys_hbm.shape[1]
    copies = load(
        [
            pltpu.make_async_copy(inputs_hbm.at[rows - w :], out_ref.at[:, 0:features], sem.at[0]),
            pltpu.make_async_copy(
                keys_hbm.at[rows - w :], out_ref.at[:, features : features + kv_width], sem.at[1]
            ),
            pltpu.make_async_copy(
                values_hbm.at[rows - w :],
                out_ref.at[:, features + kv_width : features + 2 * kv_width],
                sem.at[2],
            ),
        ]
    )
    line = iota((16, w), 0)
    segs = segs_ref[0:1, rows - w :]
    pos = pos_ref[0:1, rows - w :]
    aux = jnp.where(line == 0, segs, jnp.where(line == 1, pos >> 8, pos & 255))
    out_ref[0:16, features + 2 * kv_width :] = aux.astype(F32).astype(BF16)
    out_ref[16:, features + 2 * kv_width :] = jnp.zeros((w - 16, w), BF16)
    for copy in copies:
        copy.wait()


def last_tokens(layer_input, keys, values, segments, positions):
    width = layer_input.shape[1] + 2 * keys.shape[1] + WINDOW
    return pl.pallas_call(
        tail_kernel,
        name="last_tokens",
        in_specs=[VMEM, VMEM, HBM, HBM, HBM],
        out_specs=VMEM,
        out_shape=jax.ShapeDtypeStruct((WINDOW, width), BF16),
        scratch_shapes=[pltpu.SemaphoreType.DMA((3,))],
        compiler_params=pltpu.CompilerParams(vmem_limit_bytes=LIMIT),
    )(segments, positions, layer_input, keys, values)


def bit_reversed(n):
    bits = n.bit_length() - 1
    return [int(format(i, "b").zfill(bits)[::-1], 2) if bits else 0 for i in range(n)]


def exchange(part, axis, by):
    count = lax.axis_size(axis)
    return lax.ppermute(part, axis, [(i, i ^ by) for i in range(count)])


def forward_one(part, axis):
    count = lax.axis_size(axis)
    return lax.ppermute(part, axis, [(i, i + 1) for i in range(count - 1)])


def body(query, keys, values, grad_out, layer_input, sinks, segments, positions):
    n_dp = lax.axis_size("dp")
    n_seq = lax.axis_size("seq")
    dp_index = lax.axis_index("dp")
    seq_index = lax.axis_index("seq")
    core = seq_index & 1
    kv_width = keys.shape[2]
    features = layer_input.shape[2]
    piece = features // (2 * n_dp)

    tail = last_tokens(layer_input[0], keys[0], values[0], segments, positions)
    rim = forward_one(tail, "seq")
    local = local_grads(query[0], grad_out[0], keys[0], values[0], segments, positions, sinks)
    place = jnp.stack([dp_index, core, seq_index]).astype(jnp.int32)
    dq, send, keep = rim_grads(
        local, query[0], grad_out[0], keys[0], values[0], layer_input[0], rim, segments, sinks, place, n_dp
    )
    if piece % 16:
        plain = jnp.concatenate([keep, send], axis=0).reshape(n_dp, 2, piece, kv_width)
        plain = jnp.take(plain, jnp.asarray(bit_reversed(n_dp), jnp.int32) ^ dp_index, axis=0)
        keep = jnp.take(plain, core, axis=1).reshape(-1, kv_width)
        send = jnp.take(plain, core ^ 1, axis=1).reshape(-1, kv_width)
    total = keep.astype(F32) + exchange(send, "seq", 1).astype(F32)
    by = 1
    while by < n_dp:
        half = total.shape[0] // 2
        got = exchange(total[half:].astype(BF16), "dp", by)
        total = total[:half] + got.astype(F32)
        by *= 2
    by = 2
    while by < n_seq:
        mine = total.astype(BF16)
        total = mine.astype(F32) + exchange(mine, "seq", by).astype(F32)
        by *= 2
    other = exchange(total, "seq", 1)
    pair = jnp.where(core == 0, jnp.stack([total, other]), jnp.stack([other, total]))
    return (dq[None], pair.reshape(-1, kv_width))


def solution(mesh):
    return jax.shard_map(
        body,
        mesh=mesh,
        in_specs=(
            P("dp", "seq", None),
            P("dp", "seq", None),
            P("dp", "seq", None),
            P("dp", "seq", None),
            P("dp", "seq", None),
            P(),
            P("dp", "seq"),
            P("dp", "seq"),
        ),
        out_specs=(P("dp", "seq", None), P("dp", None)),
        check_vma=False,
    )
```

time: 174 us -> 48.7 us (0.28)
  waiting for transfers between devices: 92.7 us -> 17 us
  matrix products: 20.4 us -> 0 us
  local copies, waits for them, and re-layouts: 22 us -> 5.53 us
  between operations: 14.5 us -> 0.79 us
  other arithmetic: 13.5 us -> 0.95 us
  Pallas kernels: 0 us -> 12.1 us
  starting transfers between devices: 10.2 us -> 12.1 us
    unnamed x3 -> x0, waiting for transfers between devices: 60.4 us -> none
    psum x1 -> x0, waiting for transfers between devices: 30.6 us -> none  [body(): shard = lax.psum(shard, 'seq')]
    dot_general x17 -> x0, matrix products: 20.4 us -> none  [the longest x4 8.07 us: body(): jnp.einsum('qhd,kd->hqk', g_grp, v_grp, preferred_element_type=jnp.float32)]
    ppermute x4 -> x7, waiting for transfers between devices: 1.64 us -> 17 us  [the longest x6 17 us: exchange(): return lax.ppermute(part, axis, [(i, i ^ by) for i in range(count)])]
    pallas_call x0 -> x3, Pallas kernels: none -> 12.1 us  [the longest x1 6.03 us: local_grads(): pl.pallas_call(lambda *refs: local_kernel(n_kv, group, *refs), name='loca...]
    slice x15 -> x3, local copies, waits for them, and re-layouts: 11.4 us -> 0.04 us  [body(): got = exchange(total[half:].astype(BF16), 'dp', by)]
    convert_element_type x4 -> x1, other arithmetic: 7.44 us -> 0.01 us  [body(): mine = total.astype(BF16)]
    unnamed x35 -> x24, local copies, waits for them, and re-layouts: 9.09 us -> 5.49 us
  transfers between devices with their start and end apart: 6 -> 7, of which waited for: 3 -> 6; matrix products, arithmetic and copies ran while one was open for 17% -> 0% of each run, Pallas kernels for 0% -> 12%
where the time goes in v2:
time: 48.7 us; the launch traced here: 48.5 us
  waiting for transfers between devices  17 us (35%)
  Pallas kernels  12.1 us (25%)
  starting transfers between devices  12.1 us (25%)
  local copies, waits for them, and re-layouts  5.53 us (11%)
  other arithmetic  0.95 us (2%)
  between operations  0.79 us (2%)
    ppermute x6, waiting for transfers between devices, exchange(): return lax.ppermute(part, axis, [(i, i ^ by) for i in range(count)])  17 us
    ppermute x6, starting transfers between devices, exchange(): return lax.ppermute(part, axis, [(i, i ^ by) for i in range(count)])  9.54 us
    pallas_call x1, Pallas kernels, local_grads(): pl.pallas_call(lambda *refs: local_kernel(n_kv, group, *refs), name='loca...  6.03 us
    pallas_call x1, Pallas kernels, rim_grads(): pl.pallas_call(lambda *refs: rim_kernel(n_kv, group, n_dp, *refs), name='...  5.98 us
    unnamed x24, local copies, waits for them, and re-layouts  5.49 us
    ppermute x1, starting transfers between devices, forward_one(): return lax.ppermute(part, axis, [(i, i + 1) for i in range(count - 1)])  2.56 us
  transfers between devices with their start and end apart: 7, of which 6 were waited for; matrix products, arithmetic and copies ran while one was open for 0% of the time, Pallas kernels for 12%

profile of v2, /device:TPU:0, one launch (start us, length us, event | category | flops | bytes accessed | tf_op | source)
XLA Modules:
  0.0 48.5 jit_solution(507672832215226616)
XLA Ops:
  0.6 0.0 copy-start.9
  0.6 0.0 copy-start.8
  0.7 0.7 %copy-done.9 = s32[1,256]{1,0:T(1,128)S(1)} copy-done((s32[1,256]{1,0:T(1,128)S(1)}, s32[1,256]{1,0:T(1,128)}, u32[]{:S(2)}) %copy-start.9) | copy-done | bytes 1048
  1.3 0.0 copy-done.8
  1.3 0.0 copy-start
  1.3 1.1 %copy-done = bf16[1,256,1536]{2,1,0:T(8,128)(2,1)S(1)} copy-done((bf16[1,256,1536]{2,1,0:T(8,128)(2,1)S(1)}, bf16[1,256,1536]{2,1,0:T(8,128)(2,1)}, u32[]{:S(2)}) %copy-start) | copy-done | bytes 786456
  2.5 0.0 copy-start.4
  2.5 0.9 %copy-done.4 = bf16[1,256,256]{2,1,0:T(8,128)(2,1)S(1)} copy-done((bf16[1,256,256]{2,1,0:T(8,128)(2,1)S(1)}, bf16[1,256,256]{2,1,0:T(8,128)(2,1)}, u32[]{:S(2)}) %copy-start.4) | copy-done | bytes 131096
  3.4 0.0 copy-start.6
  3.4 0.9 %copy-done.6 = bf16[1,256,256]{2,1,0:T(8,128)(2,1)S(1)} copy-done((bf16[1,256,256]{2,1,0:T(8,128)(2,1)S(1)}, bf16[1,256,256]{2,1,0:T(8,128)(2,1)}, u32[]{:S(2)}) %copy-start.6) | copy-done | bytes 131096
  4.3 0.0 copy-start.2
  4.3 0.0 copy-start.5
  4.3 0.0 copy-start.7
  4.3 0.1 last_tokens.1
  4.4 2.6 %collective-permute-start = (bf16[128,2176]{1,0:T(8,128)(2,1)S(1)}, bf16[128,2176]{1,0:T(8,128)(2,1)S(1)}, u32[]{:S(2)}, u32[]{:S(2)}) collective-permute-start(bf16[128,2176]{1,0:T(8,128)(2,1)S(1)} %last_tokens.1), channel_id=1, source_target_pairs={{0,1},{1,2},{2,3},{4,5},{5,6},{6,7},{8,9},{9,10},{10,11},{12,13},{... | collective-permute-start | bytes 1671176 | tf_op jit(solution)/shard_map/ppermute | solution.py:492
  6.9 0.0 copy-start.10
  6.9 0.0 copy-start.11
  7.0 0.0 copy-done.2
  7.0 0.0 copy-done.5
  7.0 0.0 copy-done.7
  7.0 0.6 %copy-done.10 = f32[32]{0:T(128)S(1)} copy-done((f32[32]{0:T(128)S(1)}, f32[32]{0:T(128)}, u32[]{:S(2)}) %copy-start.10) | copy-done | bytes 152
  7.6 0.0 copy-done.11
  7.6 0.0 copy-start.3
  7.6 1.2 %copy-done.3 = bf16[1,256,2048]{2,1,0:T(8,128)(2,1)S(1)} copy-done((bf16[1,256,2048]{2,1,0:T(8,128)(2,1)S(1)}, bf16[1,256,2048]{2,1,0:T(8,128)(2,1)}, u32[]{:S(2)}) %copy-start.3) | copy-done | bytes 1048600
  8.8 0.0 copy-start.1
  8.8 6.0 %local_grads.1 = (bf16[256,2048]{1,0:T(8,128)(2,1)}, bf16[128,256]{1,0:T(8,128)(2,1)S(1)}, f32[128,256]{1,0:T(8,128)S(1)}, f32[4,128,128]{2,1,0:T(8,128)S(1)}) custom-call(f32[32]{0:T(128)S(1)} %copy-done.10, s32[1,256]{1,0:T(1,128)S(1)} %copy-done.8, s32[1,256]{1,0:T(1,128)S(1)} %copy-done.9, f32[1,128]{1,0:T(1,128)S(1)} %copy-done.11, ...), custom_call_target="tpu_custom_call" | custom-call | flops 671088640 | bytes 1572864 | tf_op jit(solution)/shard_map/local_grads/pallas_call | solution.py:371
  14.9 0.1 pad_add_fusion.refs_0_
  15.0 0.0 collective-permute-done.refs_12_
  15.0 0.0 copy-done.1
  15.0 6.0 %rim_grads.1 = (bf16[256,2048]{1,0:T(8,128)(2,1)}, bf16[768,256]{1,0:T(8,128)(2,1)S(1)}, bf16[768,256]{1,0:T(8,128)(2,1)S(1)}) custom-call(s32[3]{0:T(128)S(1)} %pad_add_fusion.refs_0_, f32[32]{0:T(128)S(1)} %copy-done.10, s32[1,256]{1,0:T(1,128)S(1)} %copy-done.8, f32[1,128]{1,0:T(1,128)S(1)} %copy-done.11, ...), custom_call_target="tpu_custom_call", output_to_operand_aliasing={{0}: (13, {})} | custom-call | flops 973078528 | bytes 4718592 | tf_op jit(solution)/shard_map/rim_grads/pallas_call | solution.py:408
  21.0 2.7 %collective-permute-start.1 = (bf16[768,256]{1,0:T(8,128)(2,1)S(1)}, bf16[768,256]{1,0:T(8,128)(2,1)S(1)}, u32[]{:S(2)}, u32[]{:S(2)}) collective-permute-start(bf16[768,256]{1,0:T(8,128)(2,1)S(1)} %get-tuple-element.15), channel_id=1, source_target_pairs={{0,1},{1,0},{2,3},{3,2},{4,5},{5,4},{6,7},{7,6},{8,9},{9,8},{10,11... | collective-permute-start | bytes 1179656 | tf_op jit(solution)/shard_map/ppermute | solution.py:487
  23.6 1.3 %collective-permute-done.1 = bf16[768,256]{1,0:T(8,128)(2,1)S(1)} collective-permute-done((bf16[768,256]{1,0:T(8,128)(2,1)S(1)}, bf16[768,256]{1,0:T(8,128)(2,1)S(1)}, u32[]{:S(2)}, u32[]{:S(2)}) %collective-permute-start.1) | collective-permute-done | bytes 393248 | tf_op jit(solution)/shard_map/ppermute | solution.py:487
  25.0 0.1 convert_add_fusion
  25.1 1.5 %collective-permute-start.2 = (bf16[384,256]{1,0:T(8,128)(2,1)S(1)}, bf16[384,256]{1,0:T(8,128)(2,1)S(1)}, u32[]{:S(2)}, u32[]{:S(2)}) collective-permute-start(bf16[384,256]{1,0:T(8,128)(2,1)S(1)} %slice.41), channel_id=1, source_target_pairs={{0,4},{4,0},{8,12},{12,8},{16,20},{20,16},{24,28},{28,24},{1,5},{5... | collective-permute-start | bytes 589832 | tf_op jit(solution)/shard_map/ppermute | solution.py:487
  26.7 5.7 %collective-permute-done.2 = bf16[384,256]{1,0:T(8,128)(2,1)S(1)} collective-permute-done((bf16[384,256]{1,0:T(8,128)(2,1)S(1)}, bf16[384,256]{1,0:T(8,128)(2,1)S(1)}, u32[]{:S(2)}, u32[]{:S(2)}) %collective-permute-start.2) | collective-permute-done | bytes 196640 | tf_op jit(solution)/shard_map/ppermute | solution.py:487
  32.4 1.6 %collective-permute-start.3 = (bf16[192,256]{1,0:T(8,128)(2,1)S(1)}, bf16[192,256]{1,0:T(8,128)(2,1)S(1)}, u32[]{:S(2)}, u32[]{:S(2)}) collective-permute-start(bf16[192,256]{1,0:T(8,128)(2,1)S(1)} %slice.42), channel_id=1, source_target_pairs={{0,8},{4,12},{8,0},{12,4},{16,24},{20,28},{24,16},{28,20},{1,9},{5... | collective-permute-start | bytes 294920 | tf_op jit(solution)/shard_map/ppermute | solution.py:487
  34.1 3.0 %collective-permute-done.3 = bf16[192,256]{1,0:T(8,128)(2,1)S(1)} collective-permute-done((bf16[192,256]{1,0:T(8,128)(2,1)S(1)}, bf16[192,256]{1,0:T(8,128)(2,1)S(1)}, u32[]{:S(2)}, u32[]{:S(2)}) %collective-permute-start.3) | collective-permute-done | bytes 98336 | tf_op jit(solution)/shard_map/ppermute | solution.py:487
  37.1 2.7 %collective-permute-start.4 = (bf16[96,256]{1,0:T(8,128)(2,1)S(1)}, bf16[96,256]{1,0:T(8,128)(2,1)S(1)}, u32[]{:S(2)}, u32[]{:S(2)}) collective-permute-start(bf16[96,256]{1,0:T(8,128)(2,1)S(1)} %slice.43), channel_id=1, source_target_pairs={{0,16},{4,20},{8,24},{12,28},{16,0},{20,4},{24,8},{28,12},{1,17},{... | collective-permute-start | bytes 147464 | tf_op jit(solution)/shard_map/ppermute | solution.py:487
  39.8 2.4 %collective-permute-done.4 = bf16[96,256]{1,0:T(8,128)(2,1)S(1)} collective-permute-done((bf16[96,256]{1,0:T(8,128)(2,1)S(1)}, bf16[96,256]{1,0:T(8,128)(2,1)S(1)}, u32[]{:S(2)}, u32[]{:S(2)}) %collective-permute-start.4) | collective-permute-done | bytes 49184 | tf_op jit(solution)/shard_map/ppermute | solution.py:487
  42.2 1.0 %collective-permute-start.5 = (bf16[96,256]{1,0:T(8,128)(2,1)S(1)}, bf16[96,256]{1,0:T(8,128)(2,1)S(1)}, u32[]{:S(2)}, u32[]{:S(2)}) collective-permute-start(bf16[96,256]{1,0:T(8,128)(2,1)S(1)} %fusion), channel_id=1, source_target_pairs={{0,2},{1,3},{2,0},{3,1},{4,6},{5,7},{6,4},{7,5},{8,10},{9,11},{10,... | collective-permute-start | bytes 147464 | tf_op jit(solution)/shard_map/ppermute | solution.py:487
  43.2 3.2 %collective-permute-done.5 = bf16[96,256]{1,0:T(8,128)(2,1)S(1)} collective-permute-done((bf16[96,256]{1,0:T(8,128)(2,1)S(1)}, bf16[96,256]{1,0:T(8,128)(2,1)S(1)}, u32[]{:S(2)}, u32[]{:S(2)}) %collective-permute-start.5) | collective-permute-done | bytes 49184 | tf_op jit(solution)/shard_map/ppermute | solution.py:487
  46.4 0.1 collective-permute-start.6
  46.5 1.3 %collective-permute-done.6 = f32[96,256]{1,0:T(8,128)S(1)} collective-permute-done((f32[96,256]{1,0:T(8,128)S(1)}, f32[96,256]{1,0:T(8,128)S(1)}, u32[]{:S(2)}, u32[]{:S(2)}) %collective-permute-start.6) | collective-permute-done | bytes 98336 | tf_op jit(solution)/shard_map/ppermute | solution.py:487
  47.8 0.7 %maximum_select_fusion = f32[2,96,256]{2,1,0:T(8,128)} fusion(f32[1,96,256]{2,1,0:T(8,128)S(1)} %bitcast.27, f32[1,96,256]{2,1,0:T(8,128)S(1)} %get-tuple-element.16, pred[]{:T(512)S(6)} %eq.3), kind=kLoop, calls=%fused_computation.5 | loop fusion | flops 147456 | bytes 393217 | tf_op jit(solution)/shard_map/jit(_where)/select_n | solution.py:530
  (7 shorter events, 0.1 us)
Async XLA Ops:
  0.6 0.7 %copy-start.9 = (s32[1,256]{1,0:T(1,128)S(1)}, s32[1,256]{1,0:T(1,128)}, u32[]{:S(2)}) copy-start(s32[1,256]{1,0:T(1,128)} %pos_ref.1) | copy-start | bytes 3076
  0.6 0.7 %copy-start.8 = (s32[1,256]{1,0:T(1,128)S(1)}, s32[1,256]{1,0:T(1,128)}, u32[]{:S(2)}) copy-start(s32[1,256]{1,0:T(1,128)} %refs_2_.3) | copy-start | bytes 3076
  1.3 1.1 %copy-start = (bf16[1,256,1536]{2,1,0:T(8,128)(2,1)S(1)}, bf16[1,256,1536]{2,1,0:T(8,128)(2,1)}, u32[]{:S(2)}) copy-start(bf16[1,256,1536]{2,1,0:T(8,128)(2,1)} %param.14) | copy-start | bytes 2359300
  2.5 0.9 %copy-start.4 = (bf16[1,256,256]{2,1,0:T(8,128)(2,1)S(1)}, bf16[1,256,256]{2,1,0:T(8,128)(2,1)}, u32[]{:S(2)}) copy-start(bf16[1,256,256]{2,1,0:T(8,128)(2,1)} %param.11) | copy-start | bytes 393220
  3.4 0.9 %copy-start.6 = (bf16[1,256,256]{2,1,0:T(8,128)(2,1)S(1)}, bf16[1,256,256]{2,1,0:T(8,128)(2,1)}, u32[]{:S(2)}) copy-start(bf16[1,256,256]{2,1,0:T(8,128)(2,1)} %param.12) | copy-start | bytes 393220
  4.3 2.7 %copy-start.2 = (bf16[1,256,2048]{2,1,0:T(8,128)(2,1)S(1)}, bf16[1,256,2048]{2,1,0:T(8,128)(2,1)}, u32[]{:S(2)}) copy-start(bf16[1,256,2048]{2,1,0:T(8,128)(2,1)} %param.10) | copy-start | bytes 3145732
  4.3 2.7 %copy-start.5 = (bf16[1,256,256]{2,1,0:T(8,128)(2,1)S(1)}, bf16[1,256,256]{2,1,0:T(8,128)(2,1)}, u32[]{:S(2)}) copy-start(bf16[1,256,256]{2,1,0:T(8,128)(2,1)} %param.11) | copy-start | bytes 393220
  4.3 2.7 %copy-start.7 = (bf16[1,256,256]{2,1,0:T(8,128)(2,1)S(1)}, bf16[1,256,256]{2,1,0:T(8,128)(2,1)}, u32[]{:S(2)}) copy-start(bf16[1,256,256]{2,1,0:T(8,128)(2,1)} %param.12) | copy-start | bytes 393220
  4.4 10.6 %collective-permute-start = (bf16[128,2176]{1,0:T(8,128)(2,1)S(1)}, bf16[128,2176]{1,0:T(8,128)(2,1)S(1)}, u32[]{:S(2)}, u32[]{:S(2)}) collective-permute-start(bf16[128,2176]{1,0:T(8,128)(2,1)S(1)} %last_tokens.1), channel_id=1, source_target_pairs={{0,1},{1,2},{2,3},{4,5},{5,6},{6,7},{8,9},{9,10},{10,11},{12,13},{... | collective-permute-start | bytes 1671176 | tf_op jit(solution)/shard_map/ppermute | solution.py:492
  6.9 0.7 %copy-start.10 = (f32[32]{0:T(128)S(1)}, f32[32]{0:T(128)}, u32[]{:S(2)}) copy-start(f32[32]{0:T(128)} %refs_1_.3) | copy-start | bytes 388
  6.9 0.7 %copy-start.11 = (f32[1,128]{1,0:T(1,128)S(1)}, f32[1,128]{1,0:T(1,128)}, u32[]{:S(2)}) copy-start(f32[1,128]{1,0:T(1,128)} %constant.15.clone.refs_3_) | copy-start | bytes 1540
  7.6 1.2 %copy-start.3 = (bf16[1,256,2048]{2,1,0:T(8,128)(2,1)S(1)}, bf16[1,256,2048]{2,1,0:T(8,128)(2,1)}, u32[]{:S(2)}) copy-start(bf16[1,256,2048]{2,1,0:T(8,128)(2,1)} %param.13) | copy-start | bytes 3145732
  8.8 6.1 %copy-start.1 = (bf16[1,256,1536]{2,1,0:T(8,128)(2,1)S(1)}, bf16[1,256,1536]{2,1,0:T(8,128)(2,1)}, u32[]{:S(2)}) copy-start(bf16[1,256,1536]{2,1,0:T(8,128)(2,1)} %param.14) | copy-start | bytes 2359300
  21.0 4.0 %collective-permute-start.1 = (bf16[768,256]{1,0:T(8,128)(2,1)S(1)}, bf16[768,256]{1,0:T(8,128)(2,1)S(1)}, u32[]{:S(2)}, u32[]{:S(2)}) collective-permute-start(bf16[768,256]{1,0:T(8,128)(2,1)S(1)} %get-tuple-element.15), channel_id=1, source_target_pairs={{0,1},{1,0},{2,3},{3,2},{4,5},{5,4},{6,7},{7,6},{8,9},{9,8},{10,11... | collective-permute-start | bytes 1179656 | tf_op jit(solution)/shard_map/ppermute | solution.py:487
  25.1 7.2 %collective-permute-start.2 = (bf16[384,256]{1,0:T(8,128)(2,1)S(1)}, bf16[384,256]{1,0:T(8,128)(2,1)S(1)}, u32[]{:S(2)}, u32[]{:S(2)}) collective-permute-start(bf16[384,256]{1,0:T(8,128)(2,1)S(1)} %slice.41), channel_id=1, source_target_pairs={{0,4},{4,0},{8,12},{12,8},{16,20},{20,16},{24,28},{28,24},{1,5},{5... | collective-permute-start | bytes 589832 | tf_op jit(solution)/shard_map/ppermute | solution.py:487
  32.4 4.7 %collective-permute-start.3 = (bf16[192,256]{1,0:T(8,128)(2,1)S(1)}, bf16[192,256]{1,0:T(8,128)(2,1)S(1)}, u32[]{:S(2)}, u32[]{:S(2)}) collective-permute-start(bf16[192,256]{1,0:T(8,128)(2,1)S(1)} %slice.42), channel_id=1, source_target_pairs={{0,8},{4,12},{8,0},{12,4},{16,24},{20,28},{24,16},{28,20},{1,9},{5... | collective-permute-start | bytes 294920 | tf_op jit(solution)/shard_map/ppermute | solution.py:487
  37.1 5.1 %collective-permute-start.4 = (bf16[96,256]{1,0:T(8,128)(2,1)S(1)}, bf16[96,256]{1,0:T(8,128)(2,1)S(1)}, u32[]{:S(2)}, u32[]{:S(2)}) collective-permute-start(bf16[96,256]{1,0:T(8,128)(2,1)S(1)} %slice.43), channel_id=1, source_target_pairs={{0,16},{4,20},{8,24},{12,28},{16,0},{20,4},{24,8},{28,12},{1,17},{... | collective-permute-start | bytes 147464 | tf_op jit(solution)/shard_map/ppermute | solution.py:487
  42.2 4.2 %collective-permute-start.5 = (bf16[96,256]{1,0:T(8,128)(2,1)S(1)}, bf16[96,256]{1,0:T(8,128)(2,1)S(1)}, u32[]{:S(2)}, u32[]{:S(2)}) collective-permute-start(bf16[96,256]{1,0:T(8,128)(2,1)S(1)} %fusion), channel_id=1, source_target_pairs={{0,2},{1,3},{2,0},{3,1},{4,6},{5,7},{6,4},{7,5},{8,10},{9,11},{10,... | collective-permute-start | bytes 147464 | tf_op jit(solution)/shard_map/ppermute | solution.py:487
  46.4 1.4 %collective-permute-start.6 = (f32[96,256]{1,0:T(8,128)S(1)}, f32[96,256]{1,0:T(8,128)S(1)}, u32[]{:S(2)}, u32[]{:S(2)}) collective-permute-start(f32[96,256]{1,0:T(8,128)S(1)} %get-tuple-element.17), channel_id=1, source_target_pairs={{0,1},{1,0},{2,3},{3,2},{4,5},{5,4},{6,7},{7,6},{8,9},{9,8},{10,11... | collective-permute-start | bytes 294920 | tf_op jit(solution)/shard_map/ppermute | solution.py:487
